TPU v7x, 1024 devices: a whole 4x8x16 slice. The times are simulated.
1024 devices in a mesh: shot: 32 (over x, y_hi, core), slab: 32 (over z, y_lo).
Axes of the slice: x: 4, y: 8 (y_hi: 4, y_lo: 2; y = y_hi * 2 + y_lo), z: 16, core: 2. Of those that a mesh axis runs over, the one named last changes fastest.
Arguments:
- velocity: float32 [256, 64, 128], P('slab'), may hold values from 0.2 to 0.4
- wave_state: float32 [2, 32, 2, 256, 64, 128], P(None, 'shot', None, 'slab'), may hold values from -6 to 6
- source_cells: int32 [32, 4], P('shot'), may hold values from 0 to 2097151
- source_codes: int32 [32, 4], P('shot'), may hold values from 0 to 7
- wavelets: float32 [8, 2], replicated, may hold values from -48 to 48
- receiver_cells: int32 [32, 256], P('shot'), may hold values from 0 to 2097151
- residuals: float32 [32, 2, 256], P('shot'), may hold values from -48 to 48
- momentum: float32 [256, 64, 128], P('slab', 'shot'), may hold values from -6 to 6
- diffusivity: float32 [3, 256, 64, 128], P(None, 'slab', 'shot'), may hold values from 0.02 to 0.15
Outputs:
- final_fields: float32 [32, 2, 256, 64, 128], P('shot', None, 'slab')
- new_momentum: float32 [256, 64, 128], P('slab', 'shot')
- new_velocity: float32 [256, 64, 128], P('slab', 'shot')
All inputs are finite; a program needn't handle non-finite values.
Results may differ from a plain program's by a relative error of at most 0.000076.
Values sent between devices are 32-bit elements; how exact they have to be, the bound alone decides.
A program may use at most 32 MiB of HBM per device.

v0:
```python
import math

import jax
import jax.numpy as jnp
from jax import lax
from jax.sharding import PartitionSpec as P

STENCIL_TAPS = (-205.0 / 72.0, 8.0 / 5.0, -1.0 / 5.0, 8.0 / 315.0, -1.0 / 560.0)


def with_halo(cells, sides, width):
    for axis, dim in sides:
        count = lax.axis_size(axis)
        ends = count - 1
        head = lax.slice_in_dim(cells, 0, width, axis=dim)
        tail = lax.slice_in_dim(cells, cells.shape[dim] - width, cells.shape[dim], axis=dim)
        cells = jnp.concatenate(
            [
                lax.ppermute(tail, axis, [(i, (i + 1) % count) for i in range(ends)]),
                cells,
                lax.ppermute(head, axis, [((i + 1) % count, i) for i in range(ends)]),
            ],
            axis=dim,
        )
    return cells


def laplacian(padded):
    leading = padded.ndim - 2
    lateral = jnp.pad(padded, [(0, 0)] * leading + [(4, 4), (4, 4)])
    row_count = padded.shape[-3] - 8
    size_x = padded.shape[-2]
    size_y = padded.shape[-1]

    def shifted(off_z, off_x, off_y):
        return lateral[
            ...,
            4 + off_z : 4 + off_z + row_count,
            4 + off_x : 4 + off_x + size_x,
            4 + off_y : 4 + off_y + size_y,
        ]

    summed = 3.0 * STENCIL_TAPS[0] * shifted(0, 0, 0)
    for radius in range(1, 5):
        cycle_sum = (
            shifted(radius, 0, 0)
            + shifted(-radius, 0, 0)
            + shifted(0, radius, 0)
            + shifted(0, -radius, 0)
            + shifted(0, 0, radius)
            + shifted(0, 0, -radius)
        )
        summed = summed + STENCIL_TAPS[radius] * cycle_sum
    return summed


def smooth_step(extended, kappas):
    lateral = jnp.pad(extended, ((0, 0), (0, 0), (1, 1)))
    centre = extended[1:-1, 1:-1, :]
    along_z = extended[2:, 1:-1, :] - 2.0 * centre + extended[:-2, 1:-1, :]
    along_x = extended[1:-1, 2:, :] - 2.0 * centre + extended[1:-1, :-2, :]
    along_y = lateral[1:-1, 1:-1, 2:] - 2.0 * centre + lateral[1:-1, 1:-1, :-2]
    return centre + kappas[0] * along_z + kappas[1] * along_x + kappas[2] * along_y


def point_grid(cell_ids, amounts, first_row, row_count, size_x, size_y):
    groups_here = cell_ids.shape[0]
    plane_size = size_x * size_y
    volume = row_count * plane_size
    local_ids = cell_ids - first_row * plane_size
    inside = (local_ids >= 0) & (local_ids < volume)
    offsets = jnp.arange(groups_here, dtype=jnp.int32)[:, None] * volume
    flat_index = jnp.where(inside, local_ids + offsets, groups_here * volume)
    grid = (
        jnp.zeros((groups_here * volume,), jnp.float32)
        .at[flat_index.reshape(-1)]
        .add(amounts.reshape(-1), mode="drop")
    )
    return grid.reshape(groups_here, row_count, size_x, size_y)


def on_device(
    velocity,
    wave_state,
    source_cells,
    source_codes,
    wavelets,
    receiver_cells,
    residuals,
    momentum,
    diffusivity,
):
    depth_rows = velocity.shape[0]
    size_x = velocity.shape[1]
    size_y = velocity.shape[2]
    groups_here = wave_state.shape[1]
    step_count = wavelets.shape[1]
    code_count = wavelets.shape[0]
    first_row = lax.axis_index("slab") * depth_rows
    speed_sq = velocity * velocity
    selector = (
        source_codes[:, :, None] == jnp.arange(code_count, dtype=jnp.int32)[None, None, :]
    ).astype(jnp.float32)
    amplitude = jnp.einsum("gkc,ct->gkt", selector, wavelets, precision=lax.Precision.HIGHEST)
    previous = wave_state[0]
    current = wave_state[1]
    imaging = jnp.zeros((depth_rows, size_x, size_y), jnp.float32)
    for moment in range(step_count):
        padded = with_halo(current, (("slab", 2),), 4)
        source_grid = point_grid(
            source_cells, amplitude[:, :, moment], first_row, depth_rows, size_x, size_y
        )
        rec_grid = point_grid(
            receiver_cells, residuals[:, moment, :], first_row, depth_rows, size_x, size_y
        )
        driven = speed_sq * (laplacian(padded) + jnp.stack([source_grid, rec_grid], axis=1))
        imaging = imaging + jnp.sum(driven[:, 0] * current[:, 1], axis=0)
        previous, current = (current, 2.0 * current - previous + driven)
    summed = lax.psum_scatter(imaging, "shot", scatter_dimension=1, tiled=True)
    strip_rows = summed.shape[1]
    column = lax.axis_index("shot") * strip_rows
    speed_strip = lax.dynamic_slice_in_dim(velocity, column, strip_rows, 1)
    total_groups = groups_here * lax.axis_size("shot")
    gradient = -0.2 * summed / (speed_strip * math.sqrt(total_groups * step_count))
    smoothed = gradient
    for repeat in range(2):
        extended = with_halo(smoothed, (("shot", 1), ("slab", 0)), 1)
        smoothed = smooth_step(extended, diffusivity)
    new_momentum = 0.9 * momentum + smoothed
    new_velocity = speed_strip - 0.02 * new_momentum
    return (current, new_momentum, new_velocity)


def solution(mesh):
    return jax.shard_map(
        on_device,
        mesh=mesh,
        in_specs=(
            P("slab", None, None),
            P(None, "shot", None, "slab", None, None),
            P("shot", None),
            P("shot", None),
            P(),
            P("shot", None),
            P("shot", None, None),
            P("slab", "shot", None),
            P(None, "slab", "shot", None),
        ),
        out_specs=(
            P("shot", None, "slab", None, None),
            P("slab", "shot", None),
            P("slab", "shot", None),
        ),
        check_vma=False,
    )
```

profile of v0, /device:TPU:70, one launch (start us, length us, event | category | flops | bytes accessed | tf_op | source)
XLA Modules:
  0.0 223.5 jit_solution(12249059166609633655)
XLA Ops:
  7.2 1.1 slice_bitcast_fusion
  8.4 2.6 %collective-permute-start = (f32[1,2,4,64,128]{4,3,2,1,0:T(8,128)S(1)}, f32[1,2,4,64,128]{4,3,2,1,0:T(8,128)S(1)}, u32[]{:S(2)}, u32[]{:S(2)}) collective-permute-start(f32[1,2,4,64,128]{4,3,2,1,0:T(8,128)S(1)} %get-tuple-element.18), channel_id=1, source_target_pairs={{1,0},{2,1},{3,2},{4,3},{5,4},{6,5},{7,6},{8,7},{9,8},{10,9},{11,1... | collective-permute-start | bytes 786440 | tf_op jit(solution)/shard_map/ppermute | solution.py:21
  11.0 3.3 %collective-permute-start.1 = (f32[1,2,4,64,128]{4,3,2,1,0:T(8,128)S(1)}, f32[1,2,4,64,128]{4,3,2,1,0:T(8,128)}, u32[]{:S(2)}, u32[]{:S(2)}) collective-permute-start(f32[1,2,4,64,128]{4,3,2,1,0:T(8,128)S(1)} %get-tuple-element.17), channel_id=1, source_target_pairs={{0,1},{1,2},{2,3},{3,4},{4,5},{5,6},{6,7},{7,8},{8,9},{9,10},{10,1... | collective-permute-start | bytes 786440 | tf_op jit(solution)/shard_map/ppermute | solution.py:19
  16.4 0.8 convolution_bitcast_fusion
  18.0 2.6 %scatter_custom_fusion.1 = f32[65536]{0:T(1024)} fusion(s32[256]{0:T(256)S(1)} %bitcast.64, f32[256]{0:T(256)S(1)} %bitcast.67, f32[]{:T(128)} %constant.18.clone.1), kind=kCustom, calls=%fused_computation.128 | custom fusion | flops 256 | bytes 262148 | tf_op jit(solution)/shard_map/scatter-add | solution.py:77
  20.6 1.3 scatter_custom_fusion
  21.9 2.1 collective-permute-done
  24.0 1.7 select_maximum_fusion.2
  25.7 4.5 %fusion.67 = (f32[1,2,8,64,128]{4,3,2,1,0:T(8,128)S(1)}, f32[1,2,8,64,128]{4,3,2,1,0:T(8,128)}) fusion(f32[2,1,2,8,64,128]{5,4,3,2,1,0:T(8,128)} %param.10, f32[1,1,8,64,128]{4,3,2,1,0:T(8,128)} %bitcast.61, f32[1,1,8,64,128]{4,3,2,1,0:T(8,128)} %bitcast.63, f32[1,2,16,72,136]{4,3,2,1,0:T(8,128)S(1)} %select_maximum_fusion.2, ...), kind=kLoop, calls=%fused_computation.117 | loop fusion | flops 5636096 | bytes 12320768 | tf_op jit(solution)/shard_map/add | solution.py:118
  30.3 3.5 %collective-permute-start.2 = (f32[1,2,4,64,128]{4,3,2,1,0:T(8,128)S(1)}, f32[1,2,4,64,128]{4,3,2,1,0:T(8,128)S(1)}, u32[]{:S(2)}, u32[]{:S(2)}) collective-permute-start(f32[1,2,4,64,128]{4,3,2,1,0:T(8,128)S(1)} %get-tuple-element.16), channel_id=1, source_target_pairs={{1,0},{2,1},{3,2},{4,3},{5,4},{6,5},{7,6},{8,7},{9,8},{10,9},{11,1... | collective-permute-start | bytes 786440 | tf_op jit(solution)/shard_map/ppermute | solution.py:21
  33.8 2.8 %collective-permute-start.3 = (f32[1,2,4,64,128]{4,3,2,1,0:T(8,128)S(1)}, f32[1,2,4,64,128]{4,3,2,1,0:T(8,128)}, u32[]{:S(2)}, u32[]{:S(2)}) collective-permute-start(f32[1,2,4,64,128]{4,3,2,1,0:T(8,128)S(1)} %get-tuple-element.15), channel_id=1, source_target_pairs={{0,1},{1,2},{2,3},{3,4},{4,5},{5,6},{6,7},{7,8},{8,9},{9,10},{10,1... | collective-permute-start | bytes 786440 | tf_op jit(solution)/shard_map/ppermute | solution.py:19
  36.6 2.6 %scatter_custom_fusion.3 = f32[65536]{0:T(1024)} fusion(s32[256]{0:T(256)S(1)} %bitcast.65, f32[256]{0:T(256)S(1)} %bitcast.66, f32[]{:T(128)} %constant.18.clone.1), kind=kCustom, calls=%fused_computation.124 | custom fusion | flops 256 | bytes 262148 | tf_op jit(solution)/shard_map/scatter-add | solution.py:77
  39.2 1.3 scatter_custom_fusion.2
  40.5 6.3 %collective-permute-done.2 = f32[1,2,4,64,128]{4,3,2,1,0:T(8,128)S(1)} collective-permute-done((f32[1,2,4,64,128]{4,3,2,1,0:T(8,128)S(1)}, f32[1,2,4,64,128]{4,3,2,1,0:T(8,128)S(1)}, u32[]{:S(2)}, u32[]{:S(2)}) %collective-permute-start.2) | collective-permute-done | bytes 262176 | tf_op jit(solution)/shard_map/ppermute | solution.py:21
  47.5 1.7 select_maximum_fusion
  49.2 4.5 %subtract_add_fusion = (f32[1,2,8,64,128]{4,3,2,1,0:T(8,128)}, f32[1,2,8,64,128]{4,3,2,1,0:T(8,128)}) fusion(f32[1,2,8,64,128]{4,3,2,1,0:T(8,128)S(1)} %get-tuple-element.13, f32[2,1,2,8,64,128]{5,4,3,2,1,0:T(8,128)} %param.10, f32[1,1,8,64,128]{4,3,2,1,0:T(8,128)} %bitcast.60, f32[1,1,8,64,128]{4,3,2,1,0:T(8,128)} %bitcast.62, ...), kind=kLoop, calls=%fused_computation.118 | loop fusion | flops 5636096 | bytes 11796480 | tf_op jit(solution)/shard_map/add | solution.py:118
  53.8 1.1 fusion.69
  54.9 0.9 copy.24
  55.8 0.8 constant_dynamic-slice_fusion
  56.6 120.5 %reduce-scatter.2.cloned.1.call-done = f32[8,2,128]{2,0,1:T(8,128)} async-done(((f32[8,64,128]{2,0,1:T(8,128)}), f32[8,2,128]{2,0,1:T(8,128)}) %reduce-scatter.2.cloned.1.call-update) | async-done | bytes 8208 | tf_op jit(solution)/shard_map/reduce_scatter | solution.py:119
  177.8 1.9 collective-permute-start.4
  179.7 6.7 %collective-permute-start.5 = (f32[8,1,128]{2,0,1:T(8,128)S(1)}, f32[8,1,128]{2,0,1:T(8,128)S(1)}, u32[]{:S(2)}, u32[]{:S(2)}) collective-permute-start(f32[8,1,128]{2,0,1:T(8,128)S(1)} %get-tuple-element.29), channel_id=1, source_target_pairs={{32,0},{64,32},{96,64},{128,96},{160,128},{192,160},{224,192},{256... | collective-permute-start | bytes 12296 | tf_op jit(solution)/shard_map/ppermute | solution.py:21
  186.4 1.3 collective-permute-done.5
  187.7 2.3 %collective-permute-start.6 = (f32[1,4,128]{2,0,1:T(1,128)S(1)}, f32[1,4,128]{2,0,1:T(1,128)S(1)}, u32[]{:S(2)}, u32[]{:S(2)}) collective-permute-start(f32[1,4,128]{2,0,1:T(1,128)S(1)} %get-tuple-element.25), channel_id=1, source_target_pairs={{1,0},{2,1},{3,2},{4,3},{5,4},{6,5},{7,6},{8,7},{9,8},{10,9},{11,1... | collective-permute-start | bytes 6152 | tf_op jit(solution)/shard_map/ppermute | solution.py:21
  190.0 3.5 %collective-permute-start.7 = (f32[1,4,128]{2,0,1:T(1,128)S(1)}, f32[1,4,128]{2,0,1:T(1,128)S(1)}, u32[]{:S(2)}, u32[]{:S(2)}) collective-permute-start(f32[1,4,128]{2,0,1:T(1,128)S(1)} %get-tuple-element.24), channel_id=1, source_target_pairs={{0,1},{1,2},{2,3},{3,4},{4,5},{5,6},{6,7},{7,8},{8,9},{9,10},{10,1... | collective-permute-start | bytes 6152 | tf_op jit(solution)/shard_map/ppermute | solution.py:19
  193.5 2.8 %collective-permute-done.7 = f32[1,4,128]{2,0,1:T(1,128)S(1)} collective-permute-done((f32[1,4,128]{2,0,1:T(1,128)S(1)}, f32[1,4,128]{2,0,1:T(1,128)S(1)}, u32[]{:S(2)}, u32[]{:S(2)}) %collective-permute-start.7) | collective-permute-done | bytes 2080 | tf_op jit(solution)/shard_map/ppermute | solution.py:19
  196.5 1.9 collective-permute-start.8
  198.4 6.7 %collective-permute-start.9 = (f32[8,1,128]{2,0,1:T(8,128)S(1)}, f32[8,1,128]{2,0,1:T(8,128)S(1)}, u32[]{:S(2)}, u32[]{:S(2)}) collective-permute-start(f32[8,1,128]{2,0,1:T(8,128)S(1)} %get-tuple-element.27), channel_id=1, source_target_pairs={{32,0},{64,32},{96,64},{128,96},{160,128},{192,160},{224,192},{256... | collective-permute-start | bytes 12296 | tf_op jit(solution)/shard_map/ppermute | solution.py:21
  205.1 1.3 collective-permute-done.9
  206.4 2.5 %collective-permute-start.10 = (f32[1,4,128]{2,0,1:T(1,128)S(1)}, f32[1,4,128]{2,0,1:T(1,128)S(1)}, u32[]{:S(2)}, u32[]{:S(2)}) collective-permute-start(f32[1,4,128]{2,0,1:T(1,128)S(1)} %get-tuple-element.23), channel_id=1, source_target_pairs={{1,0},{2,1},{3,2},{4,3},{5,4},{6,5},{7,6},{8,7},{9,8},{10,9},{11,1... | collective-permute-start | bytes 6152 | tf_op jit(solution)/shard_map/ppermute | solution.py:21
  208.9 3.4 %collective-permute-start.11 = (f32[1,4,128]{2,0,1:T(1,128)S(1)}, f32[1,4,128]{2,0,1:T(1,128)S(1)}, u32[]{:S(2)}, u32[]{:S(2)}) collective-permute-start(f32[1,4,128]{2,0,1:T(1,128)S(1)} %get-tuple-element.22), channel_id=1, source_target_pairs={{0,1},{1,2},{2,3},{3,4},{4,5},{5,6},{6,7},{7,8},{8,9},{9,10},{10,1... | collective-permute-start | bytes 6152 | tf_op jit(solution)/shard_map/ppermute | solution.py:19
  212.3 3.0 %collective-permute-done.11 = f32[1,4,128]{2,0,1:T(1,128)S(1)} collective-permute-done((f32[1,4,128]{2,0,1:T(1,128)S(1)}, f32[1,4,128]{2,0,1:T(1,128)S(1)}, u32[]{:S(2)}, u32[]{:S(2)}) %collective-permute-start.11) | collective-permute-done | bytes 2080 | tf_op jit(solution)/shard_map/ppermute | solution.py:19
  (39 shorter events, 6.1 us)
Async XLA Ops:
  7.2 9.2 %copy-start = (f32[8,2]{0,1:T(2,128)S(1)}, f32[8,2]{0,1:T(2,128)}, u32[]{:S(2)}) copy-start(f32[8,2]{0,1:T(2,128)} %param.13) | copy-start | bytes 196
  7.2 10.0 %copy-start.1 = (f32[8,64,128]{2,1,0:T(8,128)S(1)}, f32[8,64,128]{2,1,0:T(8,128)}, u32[]{:S(2)}) copy-start(f32[8,64,128]{2,1,0:T(8,128)} %param.9) | copy-start | bytes 786436
  7.2 169.9 %reduce-scatter.2.cloned.1.call-start = ((), (), s32[]{:S(2)}) async-start(), calls=%async_computation.1 | async-start | bytes 270336 | tf_op jit(solution)/shard_map/reduce_scatter | solution.py:119
  8.4 15.6 %collective-permute-start = (f32[1,2,4,64,128]{4,3,2,1,0:T(8,128)S(1)}, f32[1,2,4,64,128]{4,3,2,1,0:T(8,128)S(1)}, u32[]{:S(2)}, u32[]{:S(2)}) collective-permute-start(f32[1,2,4,64,128]{4,3,2,1,0:T(8,128)S(1)} %get-tuple-element.18), channel_id=1, source_target_pairs={{1,0},{2,1},{3,2},{4,3},{5,4},{6,5},{7,6},{8,7},{9,8},{10,9},{11,1... | collective-permute-start | bytes 786440 | tf_op jit(solution)/shard_map/ppermute | solution.py:21
  11.0 13.0 %collective-permute-start.1 = (f32[1,2,4,64,128]{4,3,2,1,0:T(8,128)S(1)}, f32[1,2,4,64,128]{4,3,2,1,0:T(8,128)}, u32[]{:S(2)}, u32[]{:S(2)}) collective-permute-start(f32[1,2,4,64,128]{4,3,2,1,0:T(8,128)S(1)} %get-tuple-element.17), channel_id=1, source_target_pairs={{0,1},{1,2},{2,3},{3,4},{4,5},{5,6},{6,7},{7,8},{8,9},{9,10},{10,1... | collective-permute-start | bytes 786440 | tf_op jit(solution)/shard_map/ppermute | solution.py:19
  24.0 1.7 copy-start.2
  30.3 16.5 %collective-permute-start.2 = (f32[1,2,4,64,128]{4,3,2,1,0:T(8,128)S(1)}, f32[1,2,4,64,128]{4,3,2,1,0:T(8,128)S(1)}, u32[]{:S(2)}, u32[]{:S(2)}) collective-permute-start(f32[1,2,4,64,128]{4,3,2,1,0:T(8,128)S(1)} %get-tuple-element.16), channel_id=1, source_target_pairs={{1,0},{2,1},{3,2},{4,3},{5,4},{6,5},{7,6},{8,7},{9,8},{10,9},{11,1... | collective-permute-start | bytes 786440 | tf_op jit(solution)/shard_map/ppermute | solution.py:21
  33.8 13.7 %collective-permute-start.3 = (f32[1,2,4,64,128]{4,3,2,1,0:T(8,128)S(1)}, f32[1,2,4,64,128]{4,3,2,1,0:T(8,128)}, u32[]{:S(2)}, u32[]{:S(2)}) collective-permute-start(f32[1,2,4,64,128]{4,3,2,1,0:T(8,128)S(1)} %get-tuple-element.15), channel_id=1, source_target_pairs={{0,1},{1,2},{2,3},{3,4},{4,5},{5,6},{6,7},{7,8},{8,9},{9,10},{10,1... | collective-permute-start | bytes 786440 | tf_op jit(solution)/shard_map/ppermute | solution.py:19
  46.8 0.7 copy-start.3
  49.2 144.3 %copy-start.4 = (f32[3,8,2,128]{3,2,1,0:T(2,128)S(1)}, f32[3,8,2,128]{3,2,1,0:T(2,128)}, u32[]{:S(2)}) copy-start(f32[3,8,2,128]{3,2,1,0:T(2,128)} %param.17) | copy-start | bytes 73732
  53.7 161.6 %copy-start.5 = (f32[8,2,128]{2,1,0:T(2,128)S(1)}, f32[8,2,128]{2,1,0:T(2,128)}, u32[]{:S(2)}) copy-start(f32[8,2,128]{2,1,0:T(2,128)} %param.16) | copy-start | bytes 24580
  177.8 8.6 %collective-permute-start.4 = (f32[8,1,128]{2,0,1:T(8,128)S(1)}, f32[8,1,128]{2,0,1:T(8,128)S(1)}, u32[]{:S(2)}, u32[]{:S(2)}) collective-permute-start(f32[8,1,128]{2,0,1:T(8,128)S(1)} %get-tuple-element.28), channel_id=1, source_target_pairs={{0,32},{32,64},{64,96},{96,128},{128,160},{160,192},{192,224},{224... | collective-permute-start | bytes 12296 | tf_op jit(solution)/shard_map/ppermute | solution.py:19
  179.7 8.0 %collective-permute-start.5 = (f32[8,1,128]{2,0,1:T(8,128)S(1)}, f32[8,1,128]{2,0,1:T(8,128)S(1)}, u32[]{:S(2)}, u32[]{:S(2)}) collective-permute-start(f32[8,1,128]{2,0,1:T(8,128)S(1)} %get-tuple-element.29), channel_id=1, source_target_pairs={{32,0},{64,32},{96,64},{128,96},{160,128},{192,160},{224,192},{256... | collective-permute-start | bytes 12296 | tf_op jit(solution)/shard_map/ppermute | solution.py:21
  187.7 5.9 %collective-permute-start.6 = (f32[1,4,128]{2,0,1:T(1,128)S(1)}, f32[1,4,128]{2,0,1:T(1,128)S(1)}, u32[]{:S(2)}, u32[]{:S(2)}) collective-permute-start(f32[1,4,128]{2,0,1:T(1,128)S(1)} %get-tuple-element.25), channel_id=1, source_target_pairs={{1,0},{2,1},{3,2},{4,3},{5,4},{6,5},{7,6},{8,7},{9,8},{10,9},{11,1... | collective-permute-start | bytes 6152 | tf_op jit(solution)/shard_map/ppermute | solution.py:21
  190.0 6.4 %collective-permute-start.7 = (f32[1,4,128]{2,0,1:T(1,128)S(1)}, f32[1,4,128]{2,0,1:T(1,128)S(1)}, u32[]{:S(2)}, u32[]{:S(2)}) collective-permute-start(f32[1,4,128]{2,0,1:T(1,128)S(1)} %get-tuple-element.24), channel_id=1, source_target_pairs={{0,1},{1,2},{2,3},{3,4},{4,5},{5,6},{6,7},{7,8},{8,9},{9,10},{10,1... | collective-permute-start | bytes 6152 | tf_op jit(solution)/shard_map/ppermute | solution.py:19
  196.5 8.6 %collective-permute-start.8 = (f32[8,1,128]{2,0,1:T(8,128)S(1)}, f32[8,1,128]{2,0,1:T(8,128)S(1)}, u32[]{:S(2)}, u32[]{:S(2)}) collective-permute-start(f32[8,1,128]{2,0,1:T(8,128)S(1)} %get-tuple-element.26), channel_id=1, source_target_pairs={{0,32},{32,64},{64,96},{96,128},{128,160},{160,192},{192,224},{224... | collective-permute-start | bytes 12296 | tf_op jit(solution)/shard_map/ppermute | solution.py:19
  198.4 8.0 %collective-permute-start.9 = (f32[8,1,128]{2,0,1:T(8,128)S(1)}, f32[8,1,128]{2,0,1:T(8,128)S(1)}, u32[]{:S(2)}, u32[]{:S(2)}) collective-permute-start(f32[8,1,128]{2,0,1:T(8,128)S(1)} %get-tuple-element.27), channel_id=1, source_target_pairs={{32,0},{64,32},{96,64},{128,96},{160,128},{192,160},{224,192},{256... | collective-permute-start | bytes 12296 | tf_op jit(solution)/shard_map/ppermute | solution.py:21
  206.4 5.8 %collective-permute-start.10 = (f32[1,4,128]{2,0,1:T(1,128)S(1)}, f32[1,4,128]{2,0,1:T(1,128)S(1)}, u32[]{:S(2)}, u32[]{:S(2)}) collective-permute-start(f32[1,4,128]{2,0,1:T(1,128)S(1)} %get-tuple-element.23), channel_id=1, source_target_pairs={{1,0},{2,1},{3,2},{4,3},{5,4},{6,5},{7,6},{8,7},{9,8},{10,9},{11,1... | collective-permute-start | bytes 6152 | tf_op jit(solution)/shard_map/ppermute | solution.py:21
  208.9 6.4 %collective-permute-start.11 = (f32[1,4,128]{2,0,1:T(1,128)S(1)}, f32[1,4,128]{2,0,1:T(1,128)S(1)}, u32[]{:S(2)}, u32[]{:S(2)}) collective-permute-start(f32[1,4,128]{2,0,1:T(1,128)S(1)} %get-tuple-element.22), channel_id=1, source_target_pairs={{0,1},{1,2},{2,3},{3,4},{4,5},{5,6},{6,7},{7,8},{8,9},{9,10},{10,1... | collective-permute-start | bytes 6152 | tf_op jit(solution)/shard_map/ppermute | solution.py:19
Sparse Core Ops, SparseCore 0:
  55.9 121.1 reduce-scatter.1
where the time goes:
time: 224 us
  waiting for transfers between devices  137 us (61%)
  starting transfers between devices  41 us (18%)
  other arithmetic  24.6 us (11%)
  between operations  14.3 us (6%)
  local copies, waits for them, and re-layouts  5.57 us (2%)
    reduce_scatter x1, waiting for transfers between devices, on_device(): summed = lax.psum_scatter(imaging, 'shot', scatter_dimension=1, tiled=True)  120 us
    ppermute x6, starting transfers between devices, with_halo(): lax.ppermute(head, axis, [((i + 1) % count, i) for i in range(ends)])  24.1 us
    ppermute x6, starting transfers between devices, with_halo(): lax.ppermute(tail, axis, [(i, (i + 1) % count) for i in range(ends)])  16.8 us
    ppermute x6, waiting for transfers between devices, with_halo(): lax.ppermute(head, axis, [((i + 1) % count, i) for i in range(ends)])  11 us
    add x2, other arithmetic, on_device(): previous, current = (current, 2.0 * current - previous + driven)  9.05 us
    scatter-add x4, other arithmetic, point_grid(): grid = jnp.zeros((groups_here * volume,), jnp.float32).at[flat_index.resh...  7.79 us
    ppermute x6, waiting for transfers between devices, with_halo(): lax.ppermute(tail, axis, [(i, (i + 1) % count) for i in range(ends)])  5.79 us
  transfers between devices with their start and end apart: 13, of which 7 were waited for; matrix products, arithmetic and copies ran while one was open for 5% of the time, Pallas kernels for 0%

commit v1 on v0

v1 whole, which is shorter than its diff:
```python
import math

import jax
import jax.numpy as jnp
from jax import lax
from jax.experimental import pallas as pl
from jax.experimental.pallas import tpu as pltpu
from jax.sharding import PartitionSpec as P

TAPS = (-205.0 / 72.0, 8.0 / 5.0, -1.0 / 5.0, 8.0 / 315.0, -1.0 / 560.0)
MESH = pl.DeviceIdType.MESH
ROWS, NX, NY = 8, 64, 128
SLABS, SHOTS = 32, 32
STEPS = 2
PLANE = NX * NY
SCALE = math.sqrt(SHOTS * STEPS)


def shifted(plane, offset, axis, index):
    size = plane.shape[axis]
    rolled = pltpu.roll(plane, (-offset) % size, axis)
    keep = index < size - offset if offset > 0 else index >= -offset
    return jnp.where(keep, rolled, 0.0)


def lateral(plane):
    along_x = lax.broadcasted_iota(jnp.int32, plane.shape, 0)
    along_y = lax.broadcasted_iota(jnp.int32, plane.shape, 1)
    total = (3.0 * TAPS[0]) * plane
    for r in range(1, 5):
        pairs = shifted(plane, r, 0, along_x) + shifted(plane, -r, 0, along_x)
        pairs = pairs + shifted(plane, r, 1, along_y) + shifted(plane, -r, 1, along_y)
        total = total + TAPS[r] * pairs
    return total


def kernel(
    src_cells,
    src_codes,
    wavelets,
    velocity,
    waves,
    rec_cells_hbm,
    residuals_hbm,
    momentum,
    diffusivity,
    fields,
    new_momentum,
    new_velocity,
    ext,
    prev,
    vel,
    lat,
    inject,
    rec_cells,
    residuals,
    spread,
    image,
    image_t,
    pair_in,
    pair_sum,
    group_in,
    mom,
    dif,
    held,
    around,
    load_sem,
    halo_send,
    halo_recv,
    pair_sem,
    group_send,
    group_recv,
    near_send,
    near_recv,
    ready,
):
    shot = lax.axis_index("shot")
    slab = lax.axis_index("slab")
    cx, cy, core = shot // 8, (shot // 2) % 4, shot % 2
    above, below = (slab + 1) % SLABS, (slab + SLABS - 1) % SLABS

    def at(x, y, c):
        return (x % 4) * 8 + (y % 4) * 2 + c

    partners = [(shot, above), (shot, below), (at(cx, cy, 1 - core), slab)]
    partners += [(at(cx + d, cy, core), slab) for d in (1, 2, 3)]
    partners += [(at(cx, cy + d, core), slab) for d in (1, 3)]

    loads = [
        pltpu.make_async_copy(waves.at[1, 0, 0], ext.at[0, 0, pl.ds(4, ROWS)], load_sem.at[0]),
        pltpu.make_async_copy(waves.at[1, 0, 1], ext.at[0, 1, pl.ds(4, ROWS)], load_sem.at[1]),
        pltpu.make_async_copy(rec_cells_hbm, rec_cells, load_sem.at[2]),
        pltpu.make_async_copy(residuals_hbm, residuals, load_sem.at[3]),
        pltpu.make_async_copy(velocity, vel, load_sem.at[4]),
        pltpu.make_async_copy(waves.at[0, 0], prev, load_sem.at[5]),
        pltpu.make_async_copy(momentum, mom, load_sem.at[6]),
        pltpu.make_async_copy(diffusivity, dif, load_sem.at[7]),
    ]
    barrier = pltpu.get_barrier_semaphore()

    def greet(semaphore):
        for partner in partners:
            pl.semaphore_signal(semaphore, inc=1, device_id=partner, device_id_type=MESH)

    greet(barrier)
    for load in loads:
        load.start()
    pl.semaphore_wait(barrier, len(partners))

    def halo(step, field):
        copies = []
        for way, (target, first, landing) in enumerate(((above, 4, 0), (below, 0, 12))):
            if step == 0:
                source = waves.at[1, 0, field, pl.ds(first, 4)]
            else:
                source = ext.at[1, field, pl.ds(4 + first, 4)]
            copies.append(
                pltpu.make_async_remote_copy(
                    src_ref=source,
                    dst_ref=ext.at[step, field, pl.ds(landing, 4)],
                    send_sem=halo_send.at[step, field, way],
                    recv_sem=halo_recv.at[step, field, way],
                    device_id=(shot, target),
                    device_id_type=MESH,
                )
            )
        return copies

    def start(copies):
        for copy in copies:
            copy.start()

    def arrive(copies, step, field):
        for copy in copies:
            copy.wait_recv()

        @pl.when(slab == 0)
        def _():
            ext[step, field, pl.ds(0, 4)] = jnp.zeros((4, NX, NY), jnp.float32)

        @pl.when(slab == SLABS - 1)
        def _():
            ext[step, field, pl.ds(12, 4)] = jnp.zeros((4, NX, NY), jnp.float32)

    u0, q0 = halo(0, 0), halo(0, 1)
    start(u0)
    start(q0)
    greet(ready.at[0])

    def near_part(step, field):
        def body(z, carry):
            lat[field, z] = lateral(ext[step, field, 4 + z])
            return carry

        lax.fori_loop(0, ROWS, body, 0)

    def advance(step, field):
        def body(z, carry):
            now = ext[step, field, 4 + z]
            total = lat[field, z] + inject[field, step, z]
            for r in range(1, 5):
                total = total + TAPS[r] * (
                    ext[step, field, 4 + z + r] + ext[step, field, 4 + z - r]
                )
            drive = (vel[z] * vel[z]) * total
            before = prev[field, z] if step == 0 else ext[0, field, 4 + z]
            after = 2.0 * now - before + drive
            if step == 0:
                ext[1, field, 4 + z] = after
            else:
                fields[0, field, z] = after
            if field == 0:
                rows = pl.ds(pl.multiple_of(z * NX, NX), NX)
                product = drive * ext[step, 1, 4 + z]
                image[rows, :] = product if step == 0 else image[rows, :] + product
            return carry

        lax.fori_loop(0, ROWS, body, 0)

    base = slab * (ROWS * PLANE)
    cells = [src_cells[0, k] - base for k in range(4)]
    amounts = [[wavelets[t, src_codes[0, k]] for k in range(4)] for t in range(STEPS)]

    def source_row(z, carry):
        cell = lax.broadcasted_iota(jnp.int32, (NX, NY), 0) * NY
        cell = cell + lax.broadcasted_iota(jnp.int32, (NX, NY), 1) + z * PLANE
        grids = [jnp.zeros((NX, NY), jnp.float32) for _ in range(STEPS)]
        for k in range(4):
            here = cell == cells[k]
            for t in range(STEPS):
                grids[t] = grids[t] + jnp.where(here, amounts[t][k], 0.0)
        for t in range(STEPS):
            inject[0, t, z] = grids[t]
        return carry

    lax.fori_loop(0, ROWS, source_row, 0)

    loads[0].wait()
    near_part(0, 0)
    pl.semaphore_wait(ready.at[0], len(partners))
    greet(ready.at[1])

    loads[2].wait()
    loads[3].wait()
    cell = rec_cells[...] - base
    line = cell >> 7
    lane = cell & (NY - 1)
    count = cell.shape[1]
    for t in range(STEPS):
        here = lax.broadcasted_iota(jnp.int32, (NY, count), 0) == lane
        rest = jnp.where(here, residuals[0, pl.ds(t, 1), :], 0.0)
        for part in range(3):
            piece = rest.astype(jnp.bfloat16)
            spread[part, pl.ds(t * NY, NY), :] = piece
            rest = rest - piece.astype(jnp.float32)

    def receiver_row(z, carry):
        here = lax.broadcasted_iota(jnp.int32, (NX, count), 0) + z * NX == line
        chosen = jnp.where(here, 1.0, 0.0).astype(jnp.bfloat16)
        grid = jnp.zeros((NX, STEPS * NY), jnp.float32)
        for part in range(3):
            grid = grid + lax.dot_general(
                chosen,
                spread[part],
                (((1,), (1,)), ((), ())),
                preferred_element_type=jnp.float32,
            )
        for t in range(STEPS):
            inject[1, t, z] = grid[:, t * NY : (t + 1) * NY]
        return carry

    lax.fori_loop(0, ROWS, receiver_row, 0)
    pl.semaphore_wait(ready.at[1], len(partners))

    loads[1].wait()
    near_part(0, 1)
    loads[4].wait()
    loads[5].wait()

    arrive(u0, 0, 0)
    advance(0, 0)
    u1 = halo(1, 0)
    start(u1)
    near_part(1, 0)

    arrive(q0, 0, 1)
    advance(0, 1)
    q1 = halo(1, 1)
    start(q1)

    arrive(u1, 1, 0)
    advance(1, 0)

    def turn(i, carry):
        for inner in range(4):
            strip = image[pl.ds(i * 4 + inner, ROWS, stride=NX), :]
            image_t[i, inner // 2, inner % 2] = strip
        return carry

    lax.fori_loop(0, NX // 4, turn, 0)
    pair = pltpu.make_async_remote_copy(
        src_ref=image_t.at[:, 1 - core],
        dst_ref=pair_in,
        send_sem=pair_sem.at[0],
        recv_sem=pair_sem.at[1],
        device_id=(at(cx, cy, 1 - core), slab),
        device_id_type=MESH,
    )
    pair.start()
    near_part(1, 1)
    pair.wait_recv()

    def join(i, carry):
        pair_sum[i] = image_t[i, core] + pair_in[i]
        return carry

    lax.fori_loop(0, 16, join, 0)

    def group(k):
        tx, ty = (cx + k // 4) % 4, (cy + k % 4) % 4
        return pltpu.make_async_remote_copy(
            src_ref=pair_sum.at[tx * 4 + ty],
            dst_ref=group_in.at[k],
            send_sem=group_send.at[k],
            recv_sem=group_recv.at[k],
            device_id=(at(tx, ty, core), slab),
            device_id_type=MESH,
        )

    def send_group(k, carry):
        group(k).start()
        return carry

    lax.fori_loop(1, 16, send_group, 0)

    arrive(q1, 1, 1)
    advance(1, 1)
    loads[6].wait()
    loads[7].wait()

    def take_group(k, total):
        group(k).wait_recv()
        return total + group_in[k]

    total = lax.fori_loop(1, 16, take_group, pair_sum[cx * 4 + cy])

    depth = lax.broadcasted_iota(jnp.int32, (ROWS, NY), 0)
    along_y = lax.broadcasted_iota(jnp.int32, (ROWS, NY), 1)
    speed = []
    smooth = []
    for i in range(2):
        rows = [vel[z, pl.ds(shot * 2 + i, 1), :] for z in range(ROWS)]
        speed.append(jnp.concatenate(rows, axis=0))
        smooth.append((-0.2 * total[i]) / (speed[i] * SCALE))
    left, right = (shot + SHOTS - 1) % SHOTS, (shot + 1) % SHOTS
    for turn_no in range(2):
        for i in range(2):
            held[turn_no, i] = smooth[i]
        copies = []
        for way, target in enumerate(((shot, above), (shot, below), (right, slab), (left, slab))):
            copy = pltpu.make_async_remote_copy(
                src_ref=held.at[turn_no],
                dst_ref=around.at[turn_no, way],
                send_sem=near_send.at[turn_no, way],
                recv_sem=near_recv.at[turn_no, way],
                device_id=target,
                device_id_type=MESH,
            )
            copy.start()
            copies.append(copy)
        for copy in copies:
            copy.wait_recv()
        fresh = []
        for i in range(2):
            centre = smooth[i]
            low = jnp.where(slab > 0, around[turn_no, 0, i], 0.0)
            high = jnp.where(slab < SLABS - 1, around[turn_no, 1, i], 0.0)
            down = jnp.where(depth == 0, pltpu.roll(low, 1, 0), pltpu.roll(centre, 1, 0))
            up = jnp.where(depth == ROWS - 1, pltpu.roll(high, ROWS - 1, 0), pltpu.roll(centre, ROWS - 1, 0))
            if i == 0:
                before = jnp.where(shot > 0, around[turn_no, 2, 1], 0.0)
                after = smooth[1]
            else:
                before = smooth[0]
                after = jnp.where(shot < SHOTS - 1, around[turn_no, 3, 0], 0.0)
            along_z = up - 2.0 * centre + down
            along_x = after - 2.0 * centre + before
            sides = shifted(centre, 1, 1, along_y) + shifted(centre, -1, 1, along_y)
            fresh.append(
                centre
                + dif[0, :, i, :] * along_z
                + dif[1, :, i, :] * along_x
                + dif[2, :, i, :] * (sides - 2.0 * centre)
            )
        smooth = fresh
        for copy in copies:
            copy.wait_send()
    for i in range(2):
        updated = 0.9 * mom[:, i, :] + smooth[i]
        new_momentum[:, i, :] = updated
        new_velocity[:, i, :] = speed[i] - 0.02 * updated

    for copies in (u0, q0, u1, q1):
        for copy in copies:
            copy.wait_send()
    pair.wait_send()

    def drain_group(k, carry):
        group(k).wait_send()
        return carry

    lax.fori_loop(1, 16, drain_group, 0)


def on_device(
    velocity,
    wave_state,
    source_cells,
    source_codes,
    wavelets,
    receiver_cells,
    residuals,
    momentum,
    diffusivity,
):
    hbm = pl.BlockSpec(memory_space=pl.ANY)
    smem = pl.BlockSpec(memory_space=pltpu.SMEM)
    vmem = pl.BlockSpec(memory_space=pltpu.VMEM)
    f32 = jnp.float32
    return pl.pallas_call(
        kernel,
        out_shape=(
            jax.ShapeDtypeStruct((1, 2, ROWS, NX, NY), f32),
            jax.ShapeDtypeStruct((ROWS, 2, NY), f32),
            jax.ShapeDtypeStruct((ROWS, 2, NY), f32),
        ),
        in_specs=[smem, smem, smem] + [hbm] * 6,
        out_specs=(vmem, vmem, vmem),
        scratch_shapes=[
            pltpu.VMEM((STEPS, 2, 16, NX, NY), f32),
            pltpu.VMEM((2, ROWS, NX, NY), f32),
            pltpu.VMEM((ROWS, NX, NY), f32),
            pltpu.VMEM((2, ROWS, NX, NY), f32),
            pltpu.VMEM((2, STEPS, ROWS, NX, NY), f32),
            pltpu.VMEM(receiver_cells.shape, jnp.int32),
            pltpu.VMEM(residuals.shape, f32),
            pltpu.VMEM((3, STEPS * NY, receiver_cells.shape[1]), jnp.bfloat16),
            pltpu.VMEM((ROWS * NX, NY), f32),
            pltpu.VMEM((16, 2, 2, ROWS, NY), f32),
            pltpu.VMEM((16, 2, ROWS, NY), f32),
            pltpu.VMEM((16, 2, ROWS, NY), f32),
            pltpu.VMEM((16, 2, ROWS, NY), f32),
            pltpu.VMEM((ROWS, 2, NY), f32),
            pltpu.VMEM((3, ROWS, 2, NY), f32),
            pltpu.VMEM((2, 2, ROWS, NY), f32),
            pltpu.VMEM((2, 4, 2, ROWS, NY), f32),
            pltpu.SemaphoreType.DMA((8,)),
            pltpu.SemaphoreType.DMA((STEPS, 2, 2)),
            pltpu.SemaphoreType.DMA((STEPS, 2, 2)),
            pltpu.SemaphoreType.DMA((2,)),
            pltpu.SemaphoreType.DMA((16,)),
            pltpu.SemaphoreType.DMA((16,)),
            pltpu.SemaphoreType.DMA((2, 4)),
            pltpu.SemaphoreType.DMA((2, 4)),
            pltpu.SemaphoreType.REGULAR((2,)),
        ],
        compiler_params=pltpu.CompilerParams(collective_id=0, has_side_effects=True),
    )(
        source_cells,
        source_codes,
        wavelets.T,
        velocity,
        wave_state,
        receiver_cells,
        residuals,
        momentum,
        diffusivity,
    )


def solution(mesh):
    return jax.shard_map(
        on_device,
        mesh=mesh,
        in_specs=(
            P("slab", None, None),
            P(None, "shot", None, "slab", None, None),
            P("shot", None),
            P("shot", None),
            P(),
            P("shot", None),
            P("shot", None, None),
            P("slab", "shot", None),
            P(None, "slab", "shot", None),
        ),
        out_specs=(
            P("shot", None, "slab", None, None),
            P("slab", "shot", None),
            P("slab", "shot", None),
        ),
        check_vma=False,
    )
```

time: 224 us -> 66.8 us (0.30)
  the two profiles are of different devices: /device:TPU:70 before, /device:TPU:1 now
where the time goes in v1:
time: 66.8 us; the launch traced here: 66.6 us
  Pallas kernels  62.8 us (94%)
  local copies, waits for them, and re-layouts  3.19 us (5%)
    pallas_call x1, Pallas kernels, on_device(): pl.pallas_call(kernel, out_shape=(jax.ShapeDtypeStruct((1, 2, ROWS, NX, N...  62.8 us
    unnamed x7, local copies, waits for them, and re-layouts  3.19 us

profile of v1, /device:TPU:1, one launch (start us, length us, event | category | flops | bytes accessed | tf_op | source)
XLA Modules:
  0.0 66.6 jit_solution(7448031589126019368)
XLA Ops:
  0.6 62.8 %shard_map.112 = (f32[1,2,8,64,128]{4,3,2,1,0:T(8,128)}, f32[8,2,128]{2,1,0:T(2,128)}, f32[8,2,128]{2,1,0:T(2,128)}) custom-call(s32[1,4]{1,0:T(1,128)} %src_cells.1, s32[1,4]{1,0:T(1,128)} %src_codes.1, f32[2,8]{1,0:T(2,128)} %bitcast.1, f32[8,64,128]{2,1,0:T(8,128)} %velocity.1, f32[2,1,2,8,64,128]{5,4,3,2,1,0:T(8,128)} %waves.1, s32[1,256]{1,0:T(1,128)} %rec_cells_hbm.1, ...), custom_call_target="tpu_custom_call" | custom-call | tf_op jit(solution)/shard_map/pallas_call | solution.py:390
  63.4 0.0 copy-start.1
  63.4 1.9 %copy.15 = f32[1,2,8,64,128]{4,3,2,1,0:T(8,128)} copy(f32[1,2,8,64,128]{4,3,2,1,0:T(8,128)} %get-tuple-element.6) | data formatting | bytes 1048576
  65.3 0.0 copy-done.1
  65.3 0.0 copy-start
  65.3 0.6 copy.16
  65.9 0.1 copy-done
  66.0 0.6 copy.17
Async XLA Ops:
  63.4 1.9 %copy-start.1 = (f32[8,2,128]{2,1,0:T(2,128)S(1)}, f32[8,2,128]{2,1,0:T(2,128)}, u32[]{:S(2)}) copy-start(f32[8,2,128]{2,1,0:T(2,128)} %get-tuple-element.7) | copy-start | bytes 24580
  65.3 0.7 %copy-start = (f32[8,2,128]{2,1,0:T(2,128)S(1)}, f32[8,2,128]{2,1,0:T(2,128)}, u32[]{:S(2)}) copy-start(f32[8,2,128]{2,1,0:T(2,128)} %get-tuple-element.8) | copy-start | bytes 24580

commit v2 on v1

--- a/solution.py
+++ b/solution.py
@@ -35,9 +35,9 @@
 
 
 def kernel(
-    src_cells,
-    src_codes,
-    wavelets,
+    src_cells_hbm,
+    src_codes_hbm,
+    wavelets_hbm,
     velocity,
     waves,
     rec_cells_hbm,
@@ -47,6 +47,9 @@
     fields,
     new_momentum,
     new_velocity,
+    src_cells,
+    src_codes,
+    wavelets,
     ext,
     prev,
     vel,
@@ -77,14 +80,15 @@
     shot = lax.axis_index("shot")
     slab = lax.axis_index("slab")
     cx, cy, core = shot // 8, (shot // 2) % 4, shot % 2
-    above, below = (slab + 1) % SLABS, (slab + SLABS - 1) % SLABS
+    above, below = slab + 1, slab - 1
+    has_above, has_below = slab < SLABS - 1, slab > 0
 
     def at(x, y, c):
         return (x % 4) * 8 + (y % 4) * 2 + c
 
-    partners = [(shot, above), (shot, below), (at(cx, cy, 1 - core), slab)]
+    partners = [(at(cx, cy, 1 - core), slab)]
+    partners += [(at(cx, cy + d, core), slab) for d in (1, 3)]
     partners += [(at(cx + d, cy, core), slab) for d in (1, 2, 3)]
-    partners += [(at(cx, cy + d, core), slab) for d in (1, 3)]
 
     loads = [
         pltpu.make_async_copy(waves.at[1, 0, 0], ext.at[0, 0, pl.ds(4, ROWS)], load_sem.at[0]),
@@ -95,6 +99,9 @@
         pltpu.make_async_copy(waves.at[0, 0], prev, load_sem.at[5]),
         pltpu.make_async_copy(momentum, mom, load_sem.at[6]),
         pltpu.make_async_copy(diffusivity, dif, load_sem.at[7]),
+        pltpu.make_async_copy(src_cells_hbm, src_cells, load_sem.at[8]),
+        pltpu.make_async_copy(src_codes_hbm, src_codes, load_sem.at[9]),
+        pltpu.make_async_copy(wavelets_hbm, wavelets, load_sem.at[10]),
     ]
     barrier = pltpu.get_barrier_semaphore()
 
@@ -102,10 +109,29 @@
         for partner in partners:
             pl.semaphore_signal(semaphore, inc=1, device_id=partner, device_id_type=MESH)
 
+    def meet(target):
+        pl.semaphore_signal(barrier, inc=1, device_id=(shot, target), device_id_type=MESH)
+
+    pl.when(has_above)(lambda: meet(above))
+    pl.when(has_below)(lambda: meet(below))
     greet(barrier)
     for load in loads:
         load.start()
-    pl.semaphore_wait(barrier, len(partners))
+
+    @pl.when(slab == 0)
+    def _():
+        ext[:, :, pl.ds(0, 4)] = jnp.zeros((STEPS, 2, 4, NX, NY), jnp.float32)
+        around[:, 0] = jnp.zeros((2, 2, ROWS, NY), jnp.float32)
+
+    @pl.when(slab == SLABS - 1)
+    def _():
+        ext[:, :, pl.ds(12, 4)] = jnp.zeros((STEPS, 2, 4, NX, NY), jnp.float32)
+        around[:, 1] = jnp.zeros((2, 2, ROWS, NY), jnp.float32)
+
+    pl.semaphore_wait(
+        barrier,
+        len(partners) + has_above.astype(jnp.int32) + has_below.astype(jnp.int32),
+    )
 
     def halo(step, field):
         copies = []
@@ -127,20 +153,16 @@
         return copies
 
     def start(copies):
-        for copy in copies:
-            copy.start()
-
-    def arrive(copies, step, field):
-        for copy in copies:
-            copy.wait_recv()
-
-        @pl.when(slab == 0)
-        def _():
-            ext[step, field, pl.ds(0, 4)] = jnp.zeros((4, NX, NY), jnp.float32)
-
-        @pl.when(slab == SLABS - 1)
-        def _():
-            ext[step, field, pl.ds(12, 4)] = jnp.zeros((4, NX, NY), jnp.float32)
+        pl.when(has_above)(copies[0].start)
+        pl.when(has_below)(copies[1].start)
+
+    def arrive(copies):
+        pl.when(has_below)(copies[0].wait_recv)
+        pl.when(has_above)(copies[1].wait_recv)
+
+    def leave(copies):
+        pl.when(has_above)(copies[0].wait_send)
+        pl.when(has_below)(copies[1].wait_send)
 
     u0, q0 = halo(0, 0), halo(0, 1)
     start(u0)
@@ -177,6 +199,8 @@
 
         lax.fori_loop(0, ROWS, body, 0)
 
+    for load in loads[8:]:
+        load.wait()
     base = slab * (ROWS * PLANE)
     cells = [src_cells[0, k] - base for k in range(4)]
     amounts = [[wavelets[t, src_codes[0, k]] for k in range(4)] for t in range(STEPS)]
@@ -237,18 +261,18 @@
     loads[4].wait()
     loads[5].wait()
 
-    arrive(u0, 0, 0)
+    arrive(u0)
     advance(0, 0)
     u1 = halo(1, 0)
     start(u1)
     near_part(1, 0)
 
-    arrive(q0, 0, 1)
+    arrive(q0)
     advance(0, 1)
     q1 = halo(1, 1)
-    start(q1)
-
-    arrive(u1, 1, 0)
+    pl.when(has_above)(q1[0].start)
+
+    arrive(u1)
     advance(1, 0)
 
     def turn(i, carry):
@@ -292,8 +316,9 @@
         return carry
 
     lax.fori_loop(1, 16, send_group, 0)
-
-    arrive(q1, 1, 1)
+    pl.when(has_below)(q1[1].start)
+
+    arrive(q1)
     advance(1, 1)
     loads[6].wait()
     loads[7].wait()
@@ -326,15 +351,17 @@
                 device_id=target,
                 device_id_type=MESH,
             )
-            copy.start()
             copies.append(copy)
-        for copy in copies:
-            copy.wait_recv()
+        start(copies[:2])
+        copies[2].start()
+        copies[3].start()
+        copies[2].wait_recv()
+        copies[3].wait_recv()
+        arrive(copies[:2])
         fresh = []
         for i in range(2):
             centre = smooth[i]
-            low = jnp.where(slab > 0, around[turn_no, 0, i], 0.0)
-            high = jnp.where(slab < SLABS - 1, around[turn_no, 1, i], 0.0)
+            low, high = around[turn_no, 0, i], around[turn_no, 1, i]
             down = jnp.where(depth == 0, pltpu.roll(low, 1, 0), pltpu.roll(centre, 1, 0))
             up = jnp.where(depth == ROWS - 1, pltpu.roll(high, ROWS - 1, 0), pltpu.roll(centre, ROWS - 1, 0))
             if i == 0:
@@ -353,16 +380,16 @@
                 + dif[2, :, i, :] * (sides - 2.0 * centre)
             )
         smooth = fresh
-        for copy in copies:
-            copy.wait_send()
+        leave(copies[:2])
+        copies[2].wait_send()
+        copies[3].wait_send()
     for i in range(2):
         updated = 0.9 * mom[:, i, :] + smooth[i]
         new_momentum[:, i, :] = updated
         new_velocity[:, i, :] = speed[i] - 0.02 * updated
 
     for copies in (u0, q0, u1, q1):
-        for copy in copies:
-            copy.wait_send()
+        leave(copies)
     pair.wait_send()
 
     def drain_group(k, carry):
@@ -383,8 +410,7 @@
     momentum,
     diffusivity,
 ):
-    hbm = pl.BlockSpec(memory_space=pl.ANY)
-    smem = pl.BlockSpec(memory_space=pltpu.SMEM)
+    hbm = pl.BlockSpec(memory_space=pltpu.HBM)
     vmem = pl.BlockSpec(memory_space=pltpu.VMEM)
     f32 = jnp.float32
     return pl.pallas_call(
@@ -394,9 +420,12 @@
             jax.ShapeDtypeStruct((ROWS, 2, NY), f32),
             jax.ShapeDtypeStruct((ROWS, 2, NY), f32),
         ),
-        in_specs=[smem, smem, smem] + [hbm] * 6,
+        in_specs=[hbm] * 9,
         out_specs=(vmem, vmem, vmem),
         scratch_shapes=[
+            pltpu.SMEM(source_cells.shape, jnp.int32),
+            pltpu.SMEM(source_codes.shape, jnp.int32),
+            pltpu.SMEM(wavelets.shape[::-1], f32),
             pltpu.VMEM((STEPS, 2, 16, NX, NY), f32),
             pltpu.VMEM((2, ROWS, NX, NY), f32),
             pltpu.VMEM((ROWS, NX, NY), f32),
@@ -414,7 +443,7 @@
             pltpu.VMEM((3, ROWS, 2, NY), f32),
             pltpu.VMEM((2, 2, ROWS, NY), f32),
             pltpu.VMEM((2, 4, 2, ROWS, NY), f32),
-            pltpu.SemaphoreType.DMA((8,)),
+            pltpu.SemaphoreType.DMA((11,)),
             pltpu.SemaphoreType.DMA((STEPS, 2, 2)),
             pltpu.SemaphoreType.DMA((STEPS, 2, 2)),
             pltpu.SemaphoreType.DMA((2,)),
@@ -424,17 +453,22 @@
             pltpu.SemaphoreType.DMA((2, 4)),
             pltpu.SemaphoreType.REGULAR((2,)),
         ],
-        compiler_params=pltpu.CompilerParams(collective_id=0, has_side_effects=True),
+        compiler_params=pltpu.CompilerParams(collective_id=0, has_side_effects=True, vmem_limit_bytes=16 * 2**20),
     )(
-        source_cells,
-        source_codes,
-        wavelets.T,
-        velocity,
-        wave_state,
-        receiver_cells,
-        residuals,
-        momentum,
-        diffusivity,
+        *(
+            pltpu.with_memory_space_constraint(operand, pltpu.HBM)
+            for operand in (
+                source_cells,
+                source_codes,
+                wavelets.T,
+                velocity,
+                wave_state,
+                receiver_cells,
+                residuals,
+                momentum,
+                diffusivity,
+            )
+        )
     )
 
 

time: 66.8 us -> 53.2 us (0.80)
  the two profiles are of different devices: /device:TPU:1 before, /device:TPU:256 now
where the time goes in v2:
time: 53.2 us; the launch traced here: 53.1 us
  Pallas kernels  50.5 us (95%)
  local copies, waits for them, and re-layouts  1.99 us (4%)
  between operations  0.64 us (1%)
    pallas_call x1, Pallas kernels, on_device(): pl.pallas_call(kernel, out_shape=(jax.ShapeDtypeStruct((1, 2, ROWS, NX, N...  50.5 us
    unnamed x3, local copies, waits for them, and re-layouts  1.99 us

profile of v2, /device:TPU:256, one launch (start us, length us, event | category | flops | bytes accessed | tf_op | source)
XLA Modules:
  0.0 53.1 jit_solution(6216753237233040640)
XLA Ops:
  0.6 50.5 %shard_map.112 = (f32[1,2,8,64,128]{4,3,2,1,0:T(8,128)S(1)}, f32[8,2,128]{2,1,0:T(2,128)S(1)}, f32[8,2,128]{2,1,0:T(2,128)S(1)}) custom-call(s32[1,4]{1,0:T(1,128)} %src_cells_hbm.1, s32[1,4]{1,0:T(1,128)} %src_codes_hbm.1, f32[2,8]{1,0:T(2,128)} %bitcast.1, f32[8,64,128]{2,1,0:T(8,128)} %velocity.1, f32[2,1,2,8,64,128]{5,4,3,2,1,0:T(8,128)} %waves.1, ...), custom_call_target="tpu_custom_call" | custom-call | tf_op jit(solution)/shard_map/pallas_call | solution.py:416
  51.1 0.8 %copy.15 = f32[1,2,8,64,128]{4,3,2,1,0:T(8,128)} copy(f32[1,2,8,64,128]{4,3,2,1,0:T(8,128)S(1)} %get-tuple-element.6) | data formatting | bytes 1048576
  51.9 0.6 %copy.16 = f32[8,2,128]{2,1,0:T(2,128)} copy(f32[8,2,128]{2,1,0:T(2,128)S(1)} %get-tuple-element.7) | data formatting | bytes 16384
  52.5 0.6 %copy.17 = f32[8,2,128]{2,1,0:T(2,128)} copy(f32[8,2,128]{2,1,0:T(2,128)S(1)} %get-tuple-element.8) | data formatting | bytes 16384

commit v3 on v2

--- a/solution.py
+++ b/solution.py
@@ -65,14 +65,22 @@
     group_in,
     mom,
     dif,
+    dif_t,
+    dif_pack,
+    dif_side,
+    dif_edge,
     held,
-    around,
+    beyond_z,
+    beyond_x,
+    corner,
     load_sem,
     halo_send,
     halo_recv,
     pair_sem,
     group_send,
     group_recv,
+    dif_send,
+    dif_recv,
     near_send,
     near_recv,
     ready,
@@ -81,7 +89,9 @@
     slab = lax.axis_index("slab")
     cx, cy, core = shot // 8, (shot // 2) % 4, shot % 2
     above, below = slab + 1, slab - 1
+    left, right = shot - 1, shot + 1
     has_above, has_below = slab < SLABS - 1, slab > 0
+    has_left, has_right = shot > 0, shot < SHOTS - 1
 
     def at(x, y, c):
         return (x % 4) * 8 + (y % 4) * 2 + c
@@ -121,12 +131,24 @@
     @pl.when(slab == 0)
     def _():
         ext[:, :, pl.ds(0, 4)] = jnp.zeros((STEPS, 2, 4, NX, NY), jnp.float32)
-        around[:, 0] = jnp.zeros((2, 2, ROWS, NY), jnp.float32)
+        beyond_z[0] = jnp.zeros((2, ROWS, NY), jnp.float32)
+        corner[0] = jnp.zeros((2, ROWS, NY), jnp.float32)
 
     @pl.when(slab == SLABS - 1)
     def _():
         ext[:, :, pl.ds(12, 4)] = jnp.zeros((STEPS, 2, 4, NX, NY), jnp.float32)
-        around[:, 1] = jnp.zeros((2, 2, ROWS, NY), jnp.float32)
+        beyond_z[1] = jnp.zeros((2, ROWS, NY), jnp.float32)
+        corner[1] = jnp.zeros((2, ROWS, NY), jnp.float32)
+
+    @pl.when(shot == 0)
+    def _():
+        beyond_x[0] = jnp.zeros((2, ROWS, NY), jnp.float32)
+        corner[:, 0] = jnp.zeros((2, ROWS, NY), jnp.float32)
+
+    @pl.when(shot == SHOTS - 1)
+    def _():
+        beyond_x[1] = jnp.zeros((2, ROWS, NY), jnp.float32)
+        corner[:, 1] = jnp.zeros((2, ROWS, NY), jnp.float32)
 
     pl.semaphore_wait(
         barrier,
@@ -256,6 +278,52 @@
     lax.fori_loop(0, ROWS, receiver_row, 0)
     pl.semaphore_wait(ready.at[1], len(partners))
 
+    loads[6].wait()
+    loads[7].wait()
+    dif_pack[...] = jnp.zeros((2, ROWS, NY), jnp.float32)
+    for i in range(2):
+        for k in range(3):
+            tile = dif[k, :, i, :]
+            dif_t[i, k] = tile
+            dif_pack[0, pl.ds(3 * i + k, 1), :] = tile[ROWS - 1 :]
+            dif_pack[1, pl.ds(3 * i + k, 1), :] = tile[:1]
+
+    def near(source, landing, send_sem, recv_sem, target, goes, comes):
+        copy = pltpu.make_async_remote_copy(
+            src_ref=source,
+            dst_ref=landing,
+            send_sem=send_sem,
+            recv_sem=recv_sem,
+            device_id=target,
+            device_id_type=MESH,
+        )
+        return copy, goes, comes
+
+    dif_ways = [
+        (dif_pack.at[0], dif_edge.at[0], (shot, above), has_above, has_below),
+        (dif_pack.at[1], dif_edge.at[1], (shot, below), has_below, has_above),
+        (dif_t.at[1], dif_side.at[0], (right, slab), has_right, has_left),
+        (dif_t.at[0], dif_side.at[1], (left, slab), has_left, has_right),
+    ]
+    dif_copies = [
+        near(source, landing, dif_send.at[n], dif_recv.at[n], target, goes, comes)
+        for n, (source, landing, target, goes, comes) in enumerate(dif_ways)
+    ]
+    near_ways = [
+        (held, beyond_z.at[0], (shot, above), has_above, has_below),
+        (held, beyond_z.at[1], (shot, below), has_below, has_above),
+        (held, beyond_x.at[0], (right, slab), has_right, has_left),
+        (held, beyond_x.at[1], (left, slab), has_left, has_right),
+        (held.at[1], corner.at[0, 0], (right, above), has_right & has_above, has_left & has_below),
+        (held.at[0], corner.at[0, 1], (left, above), has_left & has_above, has_right & has_below),
+        (held.at[1], corner.at[1, 0], (right, below), has_right & has_below, has_left & has_above),
+        (held.at[0], corner.at[1, 1], (left, below), has_left & has_below, has_right & has_above),
+    ]
+    near_copies = [
+        near(source, landing, near_send.at[n], near_recv.at[n], target, goes, comes)
+        for n, (source, landing, target, goes, comes) in enumerate(near_ways)
+    ]
+
     loads[1].wait()
     near_part(0, 1)
     loads[4].wait()
@@ -265,6 +333,8 @@
     advance(0, 0)
     u1 = halo(1, 0)
     start(u1)
+    for copy, goes, _ in dif_copies:
+        pl.when(goes)(copy.start)
     near_part(1, 0)
 
     arrive(q0)
@@ -320,8 +390,8 @@
 
     arrive(q1)
     advance(1, 1)
-    loads[6].wait()
-    loads[7].wait()
+    for copy, _, comes in dif_copies:
+        pl.when(comes)(copy.wait_recv)
 
     def take_group(k, total):
         group(k).wait_recv()
@@ -337,52 +407,111 @@
         rows = [vel[z, pl.ds(shot * 2 + i, 1), :] for z in range(ROWS)]
         speed.append(jnp.concatenate(rows, axis=0))
         smooth.append((-0.2 * total[i]) / (speed[i] * SCALE))
-    left, right = (shot + SHOTS - 1) % SHOTS, (shot + 1) % SHOTS
-    for turn_no in range(2):
-        for i in range(2):
-            held[turn_no, i] = smooth[i]
-        copies = []
-        for way, target in enumerate(((shot, above), (shot, below), (right, slab), (left, slab))):
-            copy = pltpu.make_async_remote_copy(
-                src_ref=held.at[turn_no],
-                dst_ref=around.at[turn_no, way],
-                send_sem=near_send.at[turn_no, way],
-                recv_sem=near_recv.at[turn_no, way],
-                device_id=target,
-                device_id_type=MESH,
+    for i in range(2):
+        held[i] = smooth[i]
+    for n in (4, 5, 6, 7, 2, 3, 0, 1):
+        copy, goes, _ = near_copies[n]
+        pl.when(goes)(copy.start)
+
+    def step(centre, down, up, before, after, kappas):
+        sides = shifted(centre, 1, 1, along_y) + shifted(centre, -1, 1, along_y)
+        return (
+            centre
+            + kappas[0] * (up - 2.0 * centre + down)
+            + kappas[1] * (after - 2.0 * centre + before)
+            + kappas[2] * (sides - 2.0 * centre)
+        )
+
+    def down_of(centre, low):
+        return jnp.where(depth == 0, pltpu.roll(low, 1, 0), pltpu.roll(centre, 1, 0))
+
+    def up_of(centre, high):
+        last = ROWS - 1
+        return jnp.where(depth == last, pltpu.roll(high, last, 0), pltpu.roll(centre, last, 0))
+
+    own = [[dif_t[i, k] for k in range(3)] for i in range(2)]
+    side = [[dif_side[i, k] for k in range(3)] for i in range(2)]
+    edge = [
+        [
+            [jnp.broadcast_to(dif_edge[z, pl.ds(3 * i + k, 1), :], (ROWS, NY)) for k in range(3)]
+            for i in range(2)
+        ]
+        for z in range(2)
+    ]
+    for copy, _, comes in near_copies:
+        pl.when(comes)(copy.wait_recv)
+    low, high = [[beyond_z[z, i] for i in range(2)] for z in range(2)]
+    (far_left, near_left), (near_right, far_right) = [
+        [beyond_x[x, i] for i in range(2)] for x in range(2)
+    ]
+    (low_left, low_right), (high_left, high_right) = [
+        [corner[z, x] for x in range(2)] for z in range(2)
+    ]
+    before = [near_left, smooth[0]]
+    after = [smooth[1], near_right]
+    once = [
+        step(
+            smooth[i],
+            down_of(smooth[i], low[i]),
+            up_of(smooth[i], high[i]),
+            before[i],
+            after[i],
+            own[i],
+        )
+        for i in range(2)
+    ]
+    once_left = step(
+        near_left,
+        down_of(near_left, low_left),
+        up_of(near_left, high_left),
+        far_left,
+        smooth[0],
+        side[0],
+    )
+    once_right = step(
+        near_right,
+        down_of(near_right, low_right),
+        up_of(near_right, high_right),
+        smooth[1],
+        far_right,
+        side[1],
+    )
+    once_left = jnp.where(has_left, once_left, 0.0)
+    once_right = jnp.where(has_right, once_right, 0.0)
+    low_before, low_after = [low_left, low[0]], [low[1], low_right]
+    high_before, high_after = [high_left, high[0]], [high[1], high_right]
+    last = ROWS - 1
+    twice = []
+    for i in range(2):
+        once_low = step(
+            low[i],
+            pltpu.roll(low[i], 1, 0),
+            up_of(low[i], smooth[i]),
+            low_before[i],
+            low_after[i],
+            edge[0][i],
+        )
+        once_high = step(
+            high[i],
+            down_of(high[i], smooth[i]),
+            pltpu.roll(high[i], last, 0),
+            high_before[i],
+            high_after[i],
+            edge[1][i],
+        )
+        once_low = jnp.where(has_below, once_low, 0.0)
+        once_high = jnp.where(has_above, once_high, 0.0)
+        twice.append(
+            step(
+                once[i],
+                down_of(once[i], once_low),
+                up_of(once[i], once_high),
+                once_left if i == 0 else once[0],
+                once[1] if i == 0 else once_right,
+                own[i],
             )
-            copies.append(copy)
-        start(copies[:2])
-        copies[2].start()
-        copies[3].start()
-        copies[2].wait_recv()
-        copies[3].wait_recv()
-        arrive(copies[:2])
-        fresh = []
-        for i in range(2):
-            centre = smooth[i]
-            low, high = around[turn_no, 0, i], around[turn_no, 1, i]
-            down = jnp.where(depth == 0, pltpu.roll(low, 1, 0), pltpu.roll(centre, 1, 0))
-            up = jnp.where(depth == ROWS - 1, pltpu.roll(high, ROWS - 1, 0), pltpu.roll(centre, ROWS - 1, 0))
-            if i == 0:
-                before = jnp.where(shot > 0, around[turn_no, 2, 1], 0.0)
-                after = smooth[1]
-            else:
-                before = smooth[0]
-                after = jnp.where(shot < SHOTS - 1, around[turn_no, 3, 0], 0.0)
-            along_z = up - 2.0 * centre + down
-            along_x = after - 2.0 * centre + before
-            sides = shifted(centre, 1, 1, along_y) + shifted(centre, -1, 1, along_y)
-            fresh.append(
-                centre
-                + dif[0, :, i, :] * along_z
-                + dif[1, :, i, :] * along_x
-                + dif[2, :, i, :] * (sides - 2.0 * centre)
-            )
-        smooth = fresh
-        leave(copies[:2])
-        copies[2].wait_send()
-        copies[3].wait_send()
+        )
+    smooth = twice
     for i in range(2):
         updated = 0.9 * mom[:, i, :] + smooth[i]
         new_momentum[:, i, :] = updated
@@ -391,12 +520,26 @@
     for copies in (u0, q0, u1, q1):
         leave(copies)
     pair.wait_send()
+    for copy, goes, _ in dif_copies + near_copies:
+        pl.when(goes)(copy.wait_send)
 
     def drain_group(k, carry):
         group(k).wait_send()
         return carry
 
     lax.fori_loop(1, 16, drain_group, 0)
+
+
+def store(*refs):
+    sources, targets, sem = refs[:3], refs[3:6], refs[6]
+    copies = [
+        pltpu.make_async_copy(source, target, sem.at[n])
+        for n, (source, target) in enumerate(zip(sources, targets))
+    ]
+    for copy in copies:
+        copy.start()
+    for copy in copies:
+        copy.wait()
 
 
 def on_device(
@@ -413,13 +556,14 @@
     hbm = pl.BlockSpec(memory_space=pltpu.HBM)
     vmem = pl.BlockSpec(memory_space=pltpu.VMEM)
     f32 = jnp.float32
-    return pl.pallas_call(
+    results = (
+        jax.ShapeDtypeStruct((1, 2, ROWS, NX, NY), f32),
+        jax.ShapeDtypeStruct((ROWS, 2, NY), f32),
+        jax.ShapeDtypeStruct((ROWS, 2, NY), f32),
+    )
+    held = pl.pallas_call(
         kernel,
-        out_shape=(
-            jax.ShapeDtypeStruct((1, 2, ROWS, NX, NY), f32),
-            jax.ShapeDtypeStruct((ROWS, 2, NY), f32),
-            jax.ShapeDtypeStruct((ROWS, 2, NY), f32),
-        ),
+        out_shape=results,
         in_specs=[hbm] * 9,
         out_specs=(vmem, vmem, vmem),
         scratch_shapes=[
@@ -441,16 +585,24 @@
             pltpu.VMEM((16, 2, ROWS, NY), f32),
             pltpu.VMEM((ROWS, 2, NY), f32),
             pltpu.VMEM((3, ROWS, 2, NY), f32),
+            pltpu.VMEM((2, 3, ROWS, NY), f32),
+            pltpu.VMEM((2, ROWS, NY), f32),
+            pltpu.VMEM((2, 3, ROWS, NY), f32),
+            pltpu.VMEM((2, ROWS, NY), f32),
+            pltpu.VMEM((2, ROWS, NY), f32),
             pltpu.VMEM((2, 2, ROWS, NY), f32),
-            pltpu.VMEM((2, 4, 2, ROWS, NY), f32),
+            pltpu.VMEM((2, 2, ROWS, NY), f32),
+            pltpu.VMEM((2, 2, ROWS, NY), f32),
             pltpu.SemaphoreType.DMA((11,)),
             pltpu.SemaphoreType.DMA((STEPS, 2, 2)),
             pltpu.SemaphoreType.DMA((STEPS, 2, 2)),
             pltpu.SemaphoreType.DMA((2,)),
             pltpu.SemaphoreType.DMA((16,)),
             pltpu.SemaphoreType.DMA((16,)),
-            pltpu.SemaphoreType.DMA((2, 4)),
-            pltpu.SemaphoreType.DMA((2, 4)),
+            pltpu.SemaphoreType.DMA((4,)),
+            pltpu.SemaphoreType.DMA((4,)),
+            pltpu.SemaphoreType.DMA((8,)),
+            pltpu.SemaphoreType.DMA((8,)),
             pltpu.SemaphoreType.REGULAR((2,)),
         ],
         compiler_params=pltpu.CompilerParams(collective_id=0, has_side_effects=True, vmem_limit_bytes=16 * 2**20),
@@ -470,6 +622,14 @@
             )
         )
     )
+    return pl.pallas_call(
+        store,
+        out_shape=results,
+        in_specs=[vmem] * 3,
+        out_specs=(hbm,) * 3,
+        scratch_shapes=[pltpu.SemaphoreType.DMA((3,))],
+        compiler_params=pltpu.CompilerParams(vmem_limit_bytes=2**20),
+    )(*held)
 
 
 def solution(mesh):

time: 53.2 us -> 48.8 us (0.917)
  the two profiles are of different devices: /device:TPU:256 before, /device:TPU:200 now
where the time goes in v3:
time: 48.8 us; the launch traced here: 48.6 us
  Pallas kernels  48 us (98%)
  between operations  0.64 us (1%)
    pallas_call x1, Pallas kernels, on_device(): pl.pallas_call(kernel, out_shape=results, in_specs=[hbm] * 9, out_specs=(...  47.2 us

profile of v3, /device:TPU:200, one launch (start us, length us, event | category | flops | bytes accessed | tf_op | source)
XLA Modules:
  0.0 48.6 jit_solution(11253526360250179029)
XLA Ops:
  0.6 47.2 %shard_map.112 = (f32[1,2,8,64,128]{4,3,2,1,0:T(8,128)S(1)}, f32[8,2,128]{2,1,0:T(2,128)S(1)}, f32[8,2,128]{2,1,0:T(2,128)S(1)}) custom-call(s32[1,4]{1,0:T(1,128)} %src_cells_hbm.1, s32[1,4]{1,0:T(1,128)} %src_codes_hbm.1, f32[2,8]{1,0:T(2,128)} %bitcast.1, f32[8,64,128]{2,1,0:T(8,128)} %velocity.1, f32[2,1,2,8,64,128]{5,4,3,2,1,0:T(8,128)} %waves.1, ...), custom_call_target="tpu_custom_call" | custom-call | tf_op jit(solution)/shard_map/pallas_call | solution.py:564
  47.8 0.8 %shard_map.113 = (f32[1,2,8,64,128]{4,3,2,1,0:T(8,128)}, f32[8,2,128]{2,1,0:T(2,128)}, f32[8,2,128]{2,1,0:T(2,128)}) custom-call(f32[1,2,8,64,128]{4,3,2,1,0:T(8,128)S(1)} %get-tuple-element.6.refs_0_, f32[8,2,128]{2,1,0:T(2,128)S(1)} %get-tuple-element.7.refs_1_, f32[8,2,128]{2,1,0:T(2,128)S(1)} %get-tuple-element.8.refs_2_), custom_call_target="tpu_custom_call" | custom-call | tf_op jit(solution)/shard_map/pallas_call | solution.py:625

commit v4 on v3

--- a/solution.py
+++ b/solution.py
@@ -59,7 +59,7 @@
     residuals,
     spread,
     image,
-    image_t,
+    pair_out,
     pair_in,
     pair_sum,
     group_in,
@@ -155,19 +155,20 @@
         len(partners) + has_above.astype(jnp.int32) + has_below.astype(jnp.int32),
     )
 
-    def halo(step, field):
+    def halo(step, field, half):
+        across = pl.ds(half * (NX // 2), NX // 2)
         copies = []
         for way, (target, first, landing) in enumerate(((above, 4, 0), (below, 0, 12))):
             if step == 0:
-                source = waves.at[1, 0, field, pl.ds(first, 4)]
+                source = waves.at[1, 0, field, pl.ds(first, 4), across]
             else:
-                source = ext.at[1, field, pl.ds(4 + first, 4)]
+                source = ext.at[1, field, pl.ds(4 + first, 4), across]
             copies.append(
                 pltpu.make_async_remote_copy(
                     src_ref=source,
-                    dst_ref=ext.at[step, field, pl.ds(landing, 4)],
-                    send_sem=halo_send.at[step, field, way],
-                    recv_sem=halo_recv.at[step, field, way],
+                    dst_ref=ext.at[step, field, pl.ds(landing, 4), across],
+                    send_sem=halo_send.at[step, field, half, way],
+                    recv_sem=halo_recv.at[step, field, half, way],
                     device_id=(shot, target),
                     device_id_type=MESH,
                 )
@@ -186,9 +187,12 @@
         pl.when(has_above)(copies[0].wait_send)
         pl.when(has_below)(copies[1].wait_send)
 
-    u0, q0 = halo(0, 0), halo(0, 1)
-    start(u0)
-    start(q0)
+    (u0, q0), (u1, q1) = [
+        [[halo(step, field, half) for half in range(2)] for field in range(2)]
+        for step in range(STEPS)
+    ]
+    for copies in u0 + q0:
+        start(copies)
     greet(ready.at[0])
 
     def near_part(step, field):
@@ -198,24 +202,27 @@
 
         lax.fori_loop(0, ROWS, body, 0)
 
-    def advance(step, field):
+    def advance(step, field, first=0, count=NX):
+        across = pl.ds(first, count)
+
         def body(z, carry):
-            now = ext[step, field, 4 + z]
-            total = lat[field, z] + inject[field, step, z]
+            now = ext[step, field, 4 + z, across]
+            total = lat[field, z, across] + inject[field, step, z, across]
             for r in range(1, 5):
                 total = total + TAPS[r] * (
-                    ext[step, field, 4 + z + r] + ext[step, field, 4 + z - r]
+                    ext[step, field, 4 + z + r, across] + ext[step, field, 4 + z - r, across]
                 )
-            drive = (vel[z] * vel[z]) * total
-            before = prev[field, z] if step == 0 else ext[0, field, 4 + z]
+            speed_here = vel[z, across]
+            drive = (speed_here * speed_here) * total
+            before = prev[field, z, across] if step == 0 else ext[0, field, 4 + z, across]
             after = 2.0 * now - before + drive
             if step == 0:
-                ext[1, field, 4 + z] = after
+                ext[1, field, 4 + z, across] = after
             else:
-                fields[0, field, z] = after
+                fields[0, field, z, across] = after
             if field == 0:
-                rows = pl.ds(pl.multiple_of(z * NX, NX), NX)
-                product = drive * ext[step, 1, 4 + z]
+                rows = pl.ds(pl.multiple_of(z * NX + first, NX // 2), count)
+                product = drive * ext[step, 1, 4 + z, across]
                 image[rows, :] = product if step == 0 else image[rows, :] + product
             return carry
 
@@ -329,46 +336,34 @@
     loads[4].wait()
     loads[5].wait()
 
-    arrive(u0)
+    for copies in u0:
+        arrive(copies)
     advance(0, 0)
-    u1 = halo(1, 0)
-    start(u1)
+    for copies in u1:
+        start(copies)
     for copy, goes, _ in dif_copies:
         pl.when(goes)(copy.start)
     near_part(1, 0)
 
-    arrive(q0)
+    for copies in q0:
+        arrive(copies)
     advance(0, 1)
-    q1 = halo(1, 1)
-    pl.when(has_above)(q1[0].start)
-
-    arrive(u1)
-    advance(1, 0)
-
-    def turn(i, carry):
-        for inner in range(4):
-            strip = image[pl.ds(i * 4 + inner, ROWS, stride=NX), :]
-            image_t[i, inner // 2, inner % 2] = strip
-        return carry
-
-    lax.fori_loop(0, NX // 4, turn, 0)
-    pair = pltpu.make_async_remote_copy(
-        src_ref=image_t.at[:, 1 - core],
-        dst_ref=pair_in,
-        send_sem=pair_sem.at[0],
-        recv_sem=pair_sem.at[1],
-        device_id=(at(cx, cy, 1 - core), slab),
-        device_id_type=MESH,
-    )
-    pair.start()
+    pl.when(has_above)(q1[0][0].start)
     near_part(1, 1)
-    pair.wait_recv()
-
-    def join(i, carry):
-        pair_sum[i] = image_t[i, core] + pair_in[i]
-        return carry
-
-    lax.fori_loop(0, 16, join, 0)
+
+    def strip(i, c, r):
+        return image[pl.ds(i * 4 + c * 2 + r, ROWS, stride=NX), :]
+
+    def pair(half):
+        groups = pl.ds(8 * half, 8)
+        return pltpu.make_async_remote_copy(
+            src_ref=pair_out.at[groups],
+            dst_ref=pair_in.at[groups],
+            send_sem=pair_sem.at[0, half],
+            recv_sem=pair_sem.at[1, half],
+            device_id=(at(cx, cy, 1 - core), slab),
+            device_id_type=MESH,
+        )
 
     def group(k):
         tx, ty = (cx + k // 4) % 4, (cy + k % 4) % 4
@@ -381,15 +376,34 @@
             device_id_type=MESH,
         )
 
-    def send_group(k, carry):
-        group(k).start()
-        return carry
-
-    lax.fori_loop(1, 16, send_group, 0)
-    pl.when(has_below)(q1[1].start)
-
-    arrive(q1)
-    advance(1, 1)
+    for half in range(2):
+        arrive(u1[half])
+        advance(1, 0, half * (NX // 2), NX // 2)
+
+        def part(i, carry):
+            for r in range(2):
+                pair_out[i, r] = strip(i, 1 - core, r)
+            return carry
+
+        lax.fori_loop(8 * half, 8 * half + 8, part, 0, unroll=2)
+        pair(half).start()
+        pair(half).wait_recv()
+
+        def join(i, carry):
+            for r in range(2):
+                pair_sum[i, r] = strip(i, core, r) + pair_in[i, r]
+            return carry
+
+        lax.fori_loop(8 * half, 8 * half + 8, join, 0, unroll=2)
+        for dy in (2, 1, 3, 0):
+            for tx in (2 * half, 2 * half + 1):
+                k = ((tx + 4 - cx) % 4) * 4 + dy
+                if dy == 0:
+                    pl.when(tx != cx)(group(k).start)
+                else:
+                    group(k).start()
+    pl.when(has_below)(q1[0][1].start)
+    start(q1[1])
     for copy, _, comes in dif_copies:
         pl.when(comes)(copy.wait_recv)
 
@@ -412,6 +426,10 @@
     for n in (4, 5, 6, 7, 2, 3, 0, 1):
         copy, goes, _ = near_copies[n]
         pl.when(goes)(copy.start)
+
+    for copies in q1:
+        arrive(copies)
+    advance(1, 1)
 
     def step(centre, down, up, before, after, kappas):
         sides = shifted(centre, 1, 1, along_y) + shifted(centre, -1, 1, along_y)
@@ -517,9 +535,10 @@
         new_momentum[:, i, :] = updated
         new_velocity[:, i, :] = speed[i] - 0.02 * updated
 
-    for copies in (u0, q0, u1, q1):
+    for copies in u0 + q0 + u1 + q1:
         leave(copies)
-    pair.wait_send()
+    for half in range(2):
+        pair(half).wait_send()
     for copy, goes, _ in dif_copies + near_copies:
         pl.when(goes)(copy.wait_send)
 
@@ -579,7 +598,7 @@
             pltpu.VMEM(residuals.shape, f32),
             pltpu.VMEM((3, STEPS * NY, receiver_cells.shape[1]), jnp.bfloat16),
             pltpu.VMEM((ROWS * NX, NY), f32),
-            pltpu.VMEM((16, 2, 2, ROWS, NY), f32),
+            pltpu.VMEM((16, 2, ROWS, NY), f32),
             pltpu.VMEM((16, 2, ROWS, NY), f32),
             pltpu.VMEM((16, 2, ROWS, NY), f32),
             pltpu.VMEM((16, 2, ROWS, NY), f32),
@@ -594,9 +613,9 @@
             pltpu.VMEM((2, 2, ROWS, NY), f32),
             pltpu.VMEM((2, 2, ROWS, NY), f32),
             pltpu.SemaphoreType.DMA((11,)),
-            pltpu.SemaphoreType.DMA((STEPS, 2, 2)),
-            pltpu.SemaphoreType.DMA((STEPS, 2, 2)),
-            pltpu.SemaphoreType.DMA((2,)),
+            pltpu.SemaphoreType.DMA((STEPS, 2, 2, 2)),
+            pltpu.SemaphoreType.DMA((STEPS, 2, 2, 2)),
+            pltpu.SemaphoreType.DMA((2, 2)),
             pltpu.SemaphoreType.DMA((16,)),
             pltpu.SemaphoreType.DMA((16,)),
             pltpu.SemaphoreType.DMA((4,)),

time: 48.8 us -> 45.2 us (0.926)
  the two profiles are of different devices: /device:TPU:200 before, /device:TPU:206 now
where the time goes in v4:
time: 45.2 us; the launch traced here: 45.1 us
  Pallas kernels  44.4 us (98%)
  between operations  0.64 us (1%)
    pallas_call x1, Pallas kernels, on_device(): pl.pallas_call(kernel, out_shape=results, in_specs=[hbm] * 9, out_specs=(...  43.6 us

profile of v4, /device:TPU:206, one launch (start us, length us, event | category | flops | bytes accessed | tf_op | source)
XLA Modules:
  0.0 45.1 jit_solution(793252434277800458)
XLA Ops:
  0.6 43.6 %shard_map.112 = (f32[1,2,8,64,128]{4,3,2,1,0:T(8,128)S(1)}, f32[8,2,128]{2,1,0:T(2,128)S(1)}, f32[8,2,128]{2,1,0:T(2,128)S(1)}) custom-call(s32[1,4]{1,0:T(1,128)} %src_cells_hbm.1, s32[1,4]{1,0:T(1,128)} %src_codes_hbm.1, f32[2,8]{1,0:T(2,128)} %bitcast.1, f32[8,64,128]{2,1,0:T(8,128)} %velocity.1, f32[2,1,2,8,64,128]{5,4,3,2,1,0:T(8,128)} %waves.1, ...), custom_call_target="tpu_custom_call" | custom-call | tf_op jit(solution)/shard_map/pallas_call | solution.py:583
  44.2 0.8 %shard_map.113 = (f32[1,2,8,64,128]{4,3,2,1,0:T(8,128)}, f32[8,2,128]{2,1,0:T(2,128)}, f32[8,2,128]{2,1,0:T(2,128)}) custom-call(f32[1,2,8,64,128]{4,3,2,1,0:T(8,128)S(1)} %get-tuple-element.6.refs_0_, f32[8,2,128]{2,1,0:T(2,128)S(1)} %get-tuple-element.7.refs_1_, f32[8,2,128]{2,1,0:T(2,128)S(1)} %get-tuple-element.8.refs_2_), custom_call_target="tpu_custom_call" | custom-call | tf_op jit(solution)/shard_map/pallas_call | solution.py:644

commit v5 on v4

--- a/solution.py
+++ b/solution.py
@@ -12,6 +12,7 @@
 ROWS, NX, NY = 8, 64, 128
 SLABS, SHOTS = 32, 32
 STEPS = 2
+PARTS = 4
 PLANE = NX * NY
 SCALE = math.sqrt(SHOTS * STEPS)
 
@@ -155,8 +156,10 @@
         len(partners) + has_above.astype(jnp.int32) + has_below.astype(jnp.int32),
     )
 
-    def halo(step, field, half):
-        across = pl.ds(half * (NX // 2), NX // 2)
+    width = NX // PARTS
+
+    def halo(step, field, part):
+        across = pl.ds(part * width, width) if step == 1 else pl.ds(0, NX)
         copies = []
         for way, (target, first, landing) in enumerate(((above, 4, 0), (below, 0, 12))):
             if step == 0:
@@ -167,8 +170,8 @@
                 pltpu.make_async_remote_copy(
                     src_ref=source,
                     dst_ref=ext.at[step, field, pl.ds(landing, 4), across],
-                    send_sem=halo_send.at[step, field, half, way],
-                    recv_sem=halo_recv.at[step, field, half, way],
+                    send_sem=halo_send.at[step, field, part, way],
+                    recv_sem=halo_recv.at[step, field, part, way],
                     device_id=(shot, target),
                     device_id_type=MESH,
                 )
@@ -188,7 +191,7 @@
         pl.when(has_below)(copies[1].wait_send)
 
     (u0, q0), (u1, q1) = [
-        [[halo(step, field, half) for half in range(2)] for field in range(2)]
+        [[halo(step, field, part) for part in range(PARTS if step else 1)] for field in range(2)]
         for step in range(STEPS)
     ]
     for copies in u0 + q0:
@@ -221,7 +224,7 @@
             else:
                 fields[0, field, z, across] = after
             if field == 0:
-                rows = pl.ds(pl.multiple_of(z * NX + first, NX // 2), count)
+                rows = pl.ds(pl.multiple_of(z * NX + first, width), count)
                 product = drive * ext[step, 1, 4 + z, across]
                 image[rows, :] = product if step == 0 else image[rows, :] + product
             return carry
@@ -348,19 +351,19 @@
     for copies in q0:
         arrive(copies)
     advance(0, 1)
-    pl.when(has_above)(q1[0][0].start)
+    start(q1[0])
     near_part(1, 1)
 
     def strip(i, c, r):
         return image[pl.ds(i * 4 + c * 2 + r, ROWS, stride=NX), :]
 
-    def pair(half):
-        groups = pl.ds(8 * half, 8)
+    def pair(part):
+        groups = pl.ds(4 * part, 4)
         return pltpu.make_async_remote_copy(
             src_ref=pair_out.at[groups],
             dst_ref=pair_in.at[groups],
-            send_sem=pair_sem.at[0, half],
-            recv_sem=pair_sem.at[1, half],
+            send_sem=pair_sem.at[0, part],
+            recv_sem=pair_sem.at[1, part],
             device_id=(at(cx, cy, 1 - core), slab),
             device_id_type=MESH,
         )
@@ -376,34 +379,30 @@
             device_id_type=MESH,
         )
 
-    for half in range(2):
-        arrive(u1[half])
-        advance(1, 0, half * (NX // 2), NX // 2)
-
-        def part(i, carry):
+    def finish(part):
+        pair(part).wait_recv()
+        for i in range(4 * part, 4 * part + 4):
+            for r in range(2):
+                pair_sum[i, r] = strip(i, core, r) + pair_in[i, r]
+        for dy in (2, 1, 3, 0):
+            k = ((part + 4 - cx) % 4) * 4 + dy
+            if dy == 0:
+                pl.when(part != cx)(group(k).start)
+            else:
+                group(k).start()
+
+    for part in range(PARTS):
+        arrive(u1[part])
+        advance(1, 0, part * width, width)
+        for i in range(4 * part, 4 * part + 4):
             for r in range(2):
                 pair_out[i, r] = strip(i, 1 - core, r)
-            return carry
-
-        lax.fori_loop(8 * half, 8 * half + 8, part, 0, unroll=2)
-        pair(half).start()
-        pair(half).wait_recv()
-
-        def join(i, carry):
-            for r in range(2):
-                pair_sum[i, r] = strip(i, core, r) + pair_in[i, r]
-            return carry
-
-        lax.fori_loop(8 * half, 8 * half + 8, join, 0, unroll=2)
-        for dy in (2, 1, 3, 0):
-            for tx in (2 * half, 2 * half + 1):
-                k = ((tx + 4 - cx) % 4) * 4 + dy
-                if dy == 0:
-                    pl.when(tx != cx)(group(k).start)
-                else:
-                    group(k).start()
-    pl.when(has_below)(q1[0][1].start)
-    start(q1[1])
+        pair(part).start()
+        if part > 0:
+            finish(part - 1)
+    finish(PARTS - 1)
+    for copies in q1[1:]:
+        start(copies)
     for copy, _, comes in dif_copies:
         pl.when(comes)(copy.wait_recv)
 
@@ -430,6 +429,19 @@
     for copies in q1:
         arrive(copies)
     advance(1, 1)
+
+    for copies in u0 + q0 + u1 + q1:
+        leave(copies)
+    for part in range(PARTS):
+        pair(part).wait_send()
+    for copy, goes, _ in dif_copies:
+        pl.when(goes)(copy.wait_send)
+
+    def drain_group(k, carry):
+        group(k).wait_send()
+        return carry
+
+    lax.fori_loop(1, 16, drain_group, 0)
 
     def step(centre, down, up, before, after, kappas):
         sides = shifted(centre, 1, 1, along_y) + shifted(centre, -1, 1, along_y)
@@ -535,18 +547,8 @@
         new_momentum[:, i, :] = updated
         new_velocity[:, i, :] = speed[i] - 0.02 * updated
 
-    for copies in u0 + q0 + u1 + q1:
-        leave(copies)
-    for half in range(2):
-        pair(half).wait_send()
-    for copy, goes, _ in dif_copies + near_copies:
+    for copy, goes, _ in near_copies:
         pl.when(goes)(copy.wait_send)
-
-    def drain_group(k, carry):
-        group(k).wait_send()
-        return carry
-
-    lax.fori_loop(1, 16, drain_group, 0)
 
 
 def store(*refs):
@@ -613,9 +615,9 @@
             pltpu.VMEM((2, 2, ROWS, NY), f32),
             pltpu.VMEM((2, 2, ROWS, NY), f32),
             pltpu.SemaphoreType.DMA((11,)),
-            pltpu.SemaphoreType.DMA((STEPS, 2, 2, 2)),
-            pltpu.SemaphoreType.DMA((STEPS, 2, 2, 2)),
-            pltpu.SemaphoreType.DMA((2, 2)),
+            pltpu.SemaphoreType.DMA((STEPS, 2, PARTS, 2)),
+            pltpu.SemaphoreType.DMA((STEPS, 2, PARTS, 2)),
+            pltpu.SemaphoreType.DMA((2, PARTS)),
             pltpu.SemaphoreType.DMA((16,)),
             pltpu.SemaphoreType.DMA((16,)),
             pltpu.SemaphoreType.DMA((4,)),

time: 45.2 us -> 43.9 us (0.971)
  Pallas kernels: 44.4 us -> 43.1 us
    pallas_call x1, Pallas kernels: 43.6 us -> 42.2 us  [on_device(): pl.pallas_call(kernel, out_shape=results, in_specs=[hbm] * 9, out_specs=(...]
where the time goes in v5:
time: 43.9 us; the launch traced here: 43.7 us
  Pallas kernels  43.1 us (98%)
  between operations  0.64 us (1%)
    pallas_call x1, Pallas kernels, on_device(): pl.pallas_call(kernel, out_shape=results, in_specs=[hbm] * 9, out_specs=(...  42.2 us

profile of v5, /device:TPU:206, one launch (start us, length us, event | category | flops | bytes accessed | tf_op | source)
XLA Modules:
  0.0 43.7 jit_solution(14509495857553760642)
XLA Ops:
  0.6 42.2 %shard_map.112 = (f32[1,2,8,64,128]{4,3,2,1,0:T(8,128)S(1)}, f32[8,2,128]{2,1,0:T(2,128)S(1)}, f32[8,2,128]{2,1,0:T(2,128)S(1)}) custom-call(s32[1,4]{1,0:T(1,128)} %src_cells_hbm.1, s32[1,4]{1,0:T(1,128)} %src_codes_hbm.1, f32[2,8]{1,0:T(2,128)} %bitcast.1, f32[8,64,128]{2,1,0:T(8,128)} %velocity.1, f32[2,1,2,8,64,128]{5,4,3,2,1,0:T(8,128)} %waves.1, ...), custom_call_target="tpu_custom_call" | custom-call | tf_op jit(solution)/shard_map/pallas_call | solution.py:585
  42.9 0.8 %shard_map.113 = (f32[1,2,8,64,128]{4,3,2,1,0:T(8,128)}, f32[8,2,128]{2,1,0:T(2,128)}, f32[8,2,128]{2,1,0:T(2,128)}) custom-call(f32[1,2,8,64,128]{4,3,2,1,0:T(8,128)S(1)} %get-tuple-element.6.refs_0_, f32[8,2,128]{2,1,0:T(2,128)S(1)} %get-tuple-element.7.refs_1_, f32[8,2,128]{2,1,0:T(2,128)S(1)} %get-tuple-element.8.refs_2_), custom_call_target="tpu_custom_call" | custom-call | tf_op jit(solution)/shard_map/pallas_call | solution.py:646

commit v6 on v5

--- a/solution.py
+++ b/solution.py
@@ -158,8 +158,12 @@
 
     width = NX // PARTS
 
-    def halo(step, field, part):
-        across = pl.ds(part * width, width) if step == 1 else pl.ds(0, NX)
+    away = (2, 1, 3, 0)
+    quarters = [(cx + d) % 4 for d in away]
+    firsts = [pl.multiple_of(quarter * width, width) for quarter in quarters]
+
+    def halo(step, field, turn):
+        across = pl.ds(firsts[turn], width) if step == 1 else pl.ds(0, NX)
         copies = []
         for way, (target, first, landing) in enumerate(((above, 4, 0), (below, 0, 12))):
             if step == 0:
@@ -170,8 +174,8 @@
                 pltpu.make_async_remote_copy(
                     src_ref=source,
                     dst_ref=ext.at[step, field, pl.ds(landing, 4), across],
-                    send_sem=halo_send.at[step, field, part, way],
-                    recv_sem=halo_recv.at[step, field, part, way],
+                    send_sem=halo_send.at[step, field, turn, way],
+                    recv_sem=halo_recv.at[step, field, turn, way],
                     device_id=(shot, target),
                     device_id_type=MESH,
                 )
@@ -191,7 +195,7 @@
         pl.when(has_below)(copies[1].wait_send)
 
     (u0, q0), (u1, q1) = [
-        [[halo(step, field, part) for part in range(PARTS if step else 1)] for field in range(2)]
+        [[halo(step, field, turn) for turn in range(PARTS if step else 1)] for field in range(2)]
         for step in range(STEPS)
     ]
     for copies in u0 + q0:
@@ -357,13 +361,13 @@
     def strip(i, c, r):
         return image[pl.ds(i * 4 + c * 2 + r, ROWS, stride=NX), :]
 
-    def pair(part):
-        groups = pl.ds(4 * part, 4)
+    def pair(turn):
+        groups = pl.ds(4 * quarters[turn], 4)
         return pltpu.make_async_remote_copy(
             src_ref=pair_out.at[groups],
             dst_ref=pair_in.at[groups],
-            send_sem=pair_sem.at[0, part],
-            recv_sem=pair_sem.at[1, part],
+            send_sem=pair_sem.at[0, turn],
+            recv_sem=pair_sem.at[1, turn],
             device_id=(at(cx, cy, 1 - core), slab),
             device_id_type=MESH,
         )
@@ -379,27 +383,26 @@
             device_id_type=MESH,
         )
 
-    def finish(part):
-        pair(part).wait_recv()
-        for i in range(4 * part, 4 * part + 4):
+    def finish(turn):
+        pair(turn).wait_recv()
+        for m in range(4):
+            i = 4 * quarters[turn] + m
             for r in range(2):
                 pair_sum[i, r] = strip(i, core, r) + pair_in[i, r]
         for dy in (2, 1, 3, 0):
-            k = ((part + 4 - cx) % 4) * 4 + dy
-            if dy == 0:
-                pl.when(part != cx)(group(k).start)
-            else:
-                group(k).start()
-
-    for part in range(PARTS):
-        arrive(u1[part])
-        advance(1, 0, part * width, width)
-        for i in range(4 * part, 4 * part + 4):
+            if away[turn] > 0 or dy > 0:
+                group(away[turn] * 4 + dy).start()
+
+    for turn in range(PARTS):
+        arrive(u1[turn])
+        advance(1, 0, firsts[turn], width)
+        for m in range(4):
+            i = 4 * quarters[turn] + m
             for r in range(2):
                 pair_out[i, r] = strip(i, 1 - core, r)
-        pair(part).start()
-        if part > 0:
-            finish(part - 1)
+        pair(turn).start()
+        if turn > 0:
+            finish(turn - 1)
     finish(PARTS - 1)
     for copies in q1[1:]:
         start(copies)
@@ -410,7 +413,8 @@
         group(k).wait_recv()
         return total + group_in[k]
 
-    total = lax.fori_loop(1, 16, take_group, pair_sum[cx * 4 + cy])
+    total = lax.fori_loop(4, 16, take_group, pair_sum[cx * 4 + cy])
+    total = lax.fori_loop(1, 4, take_group, total)
 
     depth = lax.broadcasted_iota(jnp.int32, (ROWS, NY), 0)
     along_y = lax.broadcasted_iota(jnp.int32, (ROWS, NY), 1)
@@ -432,8 +436,8 @@
 
     for copies in u0 + q0 + u1 + q1:
         leave(copies)
-    for part in range(PARTS):
-        pair(part).wait_send()
+    for turn in range(PARTS):
+        pair(turn).wait_send()
     for copy, goes, _ in dif_copies:
         pl.when(goes)(copy.wait_send)
 

time: 43.9 us -> 43.5 us (level)
  the two profiles are of different devices: /device:TPU:206 before, /device:TPU:505 now
where the time goes in v6:
time: 43.5 us; the launch traced here: 43.4 us
  Pallas kernels  42.7 us (98%)
  between operations  0.64 us (1%)
    pallas_call x1, Pallas kernels, on_device(): pl.pallas_call(kernel, out_shape=results, in_specs=[hbm] * 9, out_specs=(...  41.9 us

profile of v6, /device:TPU:505, one launch (start us, length us, event | category | flops | bytes accessed | tf_op | source)
XLA Modules:
  0.0 43.4 jit_solution(14282348646980954410)
XLA Ops:
  0.6 41.9 %shard_map.112 = (f32[1,2,8,64,128]{4,3,2,1,0:T(8,128)S(1)}, f32[8,2,128]{2,1,0:T(2,128)S(1)}, f32[8,2,128]{2,1,0:T(2,128)S(1)}) custom-call(s32[1,4]{1,0:T(1,128)} %src_cells_hbm.1, s32[1,4]{1,0:T(1,128)} %src_codes_hbm.1, f32[2,8]{1,0:T(2,128)} %bitcast.1, f32[8,64,128]{2,1,0:T(8,128)} %velocity.1, f32[2,1,2,8,64,128]{5,4,3,2,1,0:T(8,128)} %waves.1, ...), custom_call_target="tpu_custom_call" | custom-call | tf_op jit(solution)/shard_map/pallas_call | solution.py:589
  42.5 0.8 %shard_map.113 = (f32[1,2,8,64,128]{4,3,2,1,0:T(8,128)}, f32[8,2,128]{2,1,0:T(2,128)}, f32[8,2,128]{2,1,0:T(2,128)}) custom-call(f32[1,2,8,64,128]{4,3,2,1,0:T(8,128)S(1)} %get-tuple-element.6.refs_0_, f32[8,2,128]{2,1,0:T(2,128)S(1)} %get-tuple-element.7.refs_1_, f32[8,2,128]{2,1,0:T(2,128)S(1)} %get-tuple-element.8.refs_2_), custom_call_target="tpu_custom_call" | custom-call | tf_op jit(solution)/shard_map/pallas_call | solution.py:650

commit v7 on v6

--- a/solution.py
+++ b/solution.py
@@ -63,7 +63,9 @@
     pair_out,
     pair_in,
     pair_sum,
-    group_in,
+    column_in,
+    column_sum,
+    row_in,
     mom,
     dif,
     dif_t,
@@ -78,8 +80,8 @@
     halo_send,
     halo_recv,
     pair_sem,
-    group_send,
-    group_recv,
+    column_sem,
+    row_sem,
     dif_send,
     dif_recv,
     near_send,
@@ -356,6 +358,7 @@
         arrive(copies)
     advance(0, 1)
     start(q1[0])
+    start(q1[1])
     near_part(1, 1)
 
     def strip(i, c, r):
@@ -372,16 +375,28 @@
             device_id_type=MESH,
         )
 
-    def group(k):
-        tx, ty = (cx + k // 4) % 4, (cy + k % 4) % 4
+    def column(d, turn):
         return pltpu.make_async_remote_copy(
-            src_ref=pair_sum.at[tx * 4 + ty],
-            dst_ref=group_in.at[k],
-            send_sem=group_send.at[k],
-            recv_sem=group_recv.at[k],
-            device_id=(at(tx, ty, core), slab),
+            src_ref=pair_sum.at[pl.ds(4 * quarters[turn], 4)],
+            dst_ref=column_in.at[d],
+            send_sem=column_sem.at[0, d],
+            recv_sem=column_sem.at[1, d],
+            device_id=(at(cx + d, cy, core), slab),
             device_id_type=MESH,
         )
+
+    def row(d):
+        return pltpu.make_async_remote_copy(
+            src_ref=column_sum.at[(cy + d) % 4],
+            dst_ref=row_in.at[d],
+            send_sem=row_sem.at[0, d],
+            recv_sem=row_sem.at[1, d],
+            device_id=(at(cx, cy + d, core), slab),
+            device_id_type=MESH,
+        )
+
+    columns = [column(away[turn], turn) for turn in range(PARTS - 1)]
+    crossing = [row(d) for d in (2, 1, 3)]
 
     def finish(turn):
         pair(turn).wait_recv()
@@ -389,9 +404,8 @@
             i = 4 * quarters[turn] + m
             for r in range(2):
                 pair_sum[i, r] = strip(i, core, r) + pair_in[i, r]
-        for dy in (2, 1, 3, 0):
-            if away[turn] > 0 or dy > 0:
-                group(away[turn] * 4 + dy).start()
+        if away[turn] > 0:
+            columns[turn].start()
 
     for turn in range(PARTS):
         arrive(u1[turn])
@@ -404,17 +418,22 @@
         if turn > 0:
             finish(turn - 1)
     finish(PARTS - 1)
-    for copies in q1[1:]:
+    for copy in columns:
+        copy.wait_recv()
+    for m in range(4):
+        column_sum[m] = (
+            pair_sum[4 * cx + m] + column_in[1, m] + column_in[2, m] + column_in[3, m]
+        )
+    for copy in crossing:
+        copy.start()
+    for copies in q1[2:]:
         start(copies)
     for copy, _, comes in dif_copies:
         pl.when(comes)(copy.wait_recv)
 
-    def take_group(k, total):
-        group(k).wait_recv()
-        return total + group_in[k]
-
-    total = lax.fori_loop(4, 16, take_group, pair_sum[cx * 4 + cy])
-    total = lax.fori_loop(1, 4, take_group, total)
+    for copy in crossing:
+        copy.wait_recv()
+    total = column_sum[cy] + row_in[1] + row_in[2] + row_in[3]
 
     depth = lax.broadcasted_iota(jnp.int32, (ROWS, NY), 0)
     along_y = lax.broadcasted_iota(jnp.int32, (ROWS, NY), 1)
@@ -441,11 +460,8 @@
     for copy, goes, _ in dif_copies:
         pl.when(goes)(copy.wait_send)
 
-    def drain_group(k, carry):
-        group(k).wait_send()
-        return carry
-
-    lax.fori_loop(1, 16, drain_group, 0)
+    for copy in columns + crossing:
+        copy.wait_send()
 
     def step(centre, down, up, before, after, kappas):
         sides = shifted(centre, 1, 1, along_y) + shifted(centre, -1, 1, along_y)
@@ -607,7 +623,9 @@
             pltpu.VMEM((16, 2, ROWS, NY), f32),
             pltpu.VMEM((16, 2, ROWS, NY), f32),
             pltpu.VMEM((16, 2, ROWS, NY), f32),
-            pltpu.VMEM((16, 2, ROWS, NY), f32),
+            pltpu.VMEM((4, 4, 2, ROWS, NY), f32),
+            pltpu.VMEM((4, 2, ROWS, NY), f32),
+            pltpu.VMEM((4, 2, ROWS, NY), f32),
             pltpu.VMEM((ROWS, 2, NY), f32),
             pltpu.VMEM((3, ROWS, 2, NY), f32),
             pltpu.VMEM((2, 3, ROWS, NY), f32),
@@ -622,8 +640,8 @@
             pltpu.SemaphoreType.DMA((STEPS, 2, PARTS, 2)),
             pltpu.SemaphoreType.DMA((STEPS, 2, PARTS, 2)),
             pltpu.SemaphoreType.DMA((2, PARTS)),
-            pltpu.SemaphoreType.DMA((16,)),
-            pltpu.SemaphoreType.DMA((16,)),
+            pltpu.SemaphoreType.DMA((2, 4)),
+            pltpu.SemaphoreType.DMA((2, 4)),
             pltpu.SemaphoreType.DMA((4,)),
             pltpu.SemaphoreType.DMA((4,)),
             pltpu.SemaphoreType.DMA((8,)),

time: 43.5 us -> 45.6 us (1.048)
  the two profiles are of different devices: /device:TPU:505 before, /device:TPU:249 now
where the time goes in v7:
time: 45.6 us; the launch traced here: 45.4 us
  Pallas kernels  44.8 us (98%)
  between operations  0.64 us (1%)
    pallas_call x1, Pallas kernels, on_device(): pl.pallas_call(kernel, out_shape=results, in_specs=[hbm] * 9, out_specs=(...  43.9 us

profile of v7, /device:TPU:249, one launch (start us, length us, event | category | flops | bytes accessed | tf_op | source)
XLA Modules:
  0.0 45.4 jit_solution(9786340784507782970)
XLA Ops:
  0.6 43.9 %shard_map.112 = (f32[1,2,8,64,128]{4,3,2,1,0:T(8,128)S(1)}, f32[8,2,128]{2,1,0:T(2,128)S(1)}, f32[8,2,128]{2,1,0:T(2,128)S(1)}) custom-call(s32[1,4]{1,0:T(1,128)} %src_cells_hbm.1, s32[1,4]{1,0:T(1,128)} %src_codes_hbm.1, f32[2,8]{1,0:T(2,128)} %bitcast.1, f32[8,64,128]{2,1,0:T(8,128)} %velocity.1, f32[2,1,2,8,64,128]{5,4,3,2,1,0:T(8,128)} %waves.1, ...), custom_call_target="tpu_custom_call" | custom-call | tf_op jit(solution)/shard_map/pallas_call | solution.py:605
  44.6 0.8 %shard_map.113 = (f32[1,2,8,64,128]{4,3,2,1,0:T(8,128)}, f32[8,2,128]{2,1,0:T(2,128)}, f32[8,2,128]{2,1,0:T(2,128)}) custom-call(f32[1,2,8,64,128]{4,3,2,1,0:T(8,128)S(1)} %get-tuple-element.6.refs_0_, f32[8,2,128]{2,1,0:T(2,128)S(1)} %get-tuple-element.7.refs_1_, f32[8,2,128]{2,1,0:T(2,128)S(1)} %get-tuple-element.8.refs_2_), custom_call_target="tpu_custom_call" | custom-call | tf_op jit(solution)/shard_map/pallas_call | solution.py:668

commit v8 on v6

--- a/solution.py
+++ b/solution.py
@@ -356,7 +356,6 @@
         arrive(copies)
     advance(0, 1)
     start(q1[0])
-    near_part(1, 1)
 
     def strip(i, c, r):
         return image[pl.ds(i * 4 + c * 2 + r, ROWS, stride=NX), :]
@@ -406,6 +405,7 @@
     finish(PARTS - 1)
     for copies in q1[1:]:
         start(copies)
+    near_part(1, 1)
     for copy, _, comes in dif_copies:
         pl.when(comes)(copy.wait_recv)
 

time: 43.5 us -> 43 us (0.989)
  the two profiles are of different devices: /device:TPU:505 before, /device:TPU:456 now
where the time goes in v8:
time: 43 us; the launch traced here: 42.8 us
  Pallas kernels  42.2 us (98%)
  between operations  0.64 us (1%)
    pallas_call x1, Pallas kernels, on_device(): pl.pallas_call(kernel, out_shape=results, in_specs=[hbm] * 9, out_specs=(...  41.4 us

profile of v8, /device:TPU:456, one launch (start us, length us, event | category | flops | bytes accessed | tf_op | source)
XLA Modules:
  0.0 42.8 jit_solution(13644881496438904551)
XLA Ops:
  0.6 41.4 %shard_map.112 = (f32[1,2,8,64,128]{4,3,2,1,0:T(8,128)S(1)}, f32[8,2,128]{2,1,0:T(2,128)S(1)}, f32[8,2,128]{2,1,0:T(2,128)S(1)}) custom-call(s32[1,4]{1,0:T(1,128)} %src_cells_hbm.1, s32[1,4]{1,0:T(1,128)} %src_codes_hbm.1, f32[2,8]{1,0:T(2,128)} %bitcast.1, f32[8,64,128]{2,1,0:T(8,128)} %velocity.1, f32[2,1,2,8,64,128]{5,4,3,2,1,0:T(8,128)} %waves.1, ...), custom_call_target="tpu_custom_call" | custom-call | tf_op jit(solution)/shard_map/pallas_call | solution.py:589
  42.0 0.8 %shard_map.113 = (f32[1,2,8,64,128]{4,3,2,1,0:T(8,128)}, f32[8,2,128]{2,1,0:T(2,128)}, f32[8,2,128]{2,1,0:T(2,128)}) custom-call(f32[1,2,8,64,128]{4,3,2,1,0:T(8,128)S(1)} %get-tuple-element.6.refs_0_, f32[8,2,128]{2,1,0:T(2,128)S(1)} %get-tuple-element.7.refs_1_, f32[8,2,128]{2,1,0:T(2,128)S(1)} %get-tuple-element.8.refs_2_), custom_call_target="tpu_custom_call" | custom-call | tf_op jit(solution)/shard_map/pallas_call | solution.py:650

commit v9 on v8

--- a/solution.py
+++ b/solution.py
@@ -260,6 +260,16 @@
     pl.semaphore_wait(ready.at[0], len(partners))
     greet(ready.at[1])
 
+    loads[1].wait()
+    loads[4].wait()
+    loads[5].wait()
+
+    for copies in u0:
+        arrive(copies)
+    advance(0, 0)
+    for copies in u1:
+        start(copies)
+
     loads[2].wait()
     loads[3].wait()
     cell = rec_cells[...] - base
@@ -338,16 +348,7 @@
         for n, (source, landing, target, goes, comes) in enumerate(near_ways)
     ]
 
-    loads[1].wait()
     near_part(0, 1)
-    loads[4].wait()
-    loads[5].wait()
-
-    for copies in u0:
-        arrive(copies)
-    advance(0, 0)
-    for copies in u1:
-        start(copies)
     for copy, goes, _ in dif_copies:
         pl.when(goes)(copy.start)
     near_part(1, 0)

time: 43 us -> 43.9 us (1.021)
  the two profiles are of different devices: /device:TPU:456 before, /device:TPU:249 now
where the time goes in v9:
time: 43.9 us; the launch traced here: 43.7 us
  Pallas kernels  43.1 us (98%)
  between operations  0.64 us (1%)
    pallas_call x1, Pallas kernels, on_device(): pl.pallas_call(kernel, out_shape=results, in_specs=[hbm] * 9, out_specs=(...  42.2 us

profile of v9, /device:TPU:249, one launch (start us, length us, event | category | flops | bytes accessed | tf_op | source)
XLA Modules:
  0.0 43.7 jit_solution(13979473369286586274)
XLA Ops:
  0.6 42.2 %shard_map.112 = (f32[1,2,8,64,128]{4,3,2,1,0:T(8,128)S(1)}, f32[8,2,128]{2,1,0:T(2,128)S(1)}, f32[8,2,128]{2,1,0:T(2,128)S(1)}) custom-call(s32[1,4]{1,0:T(1,128)} %src_cells_hbm.1, s32[1,4]{1,0:T(1,128)} %src_codes_hbm.1, f32[2,8]{1,0:T(2,128)} %bitcast.1, f32[8,64,128]{2,1,0:T(8,128)} %velocity.1, f32[2,1,2,8,64,128]{5,4,3,2,1,0:T(8,128)} %waves.1, ...), custom_call_target="tpu_custom_call" | custom-call | tf_op jit(solution)/shard_map/pallas_call | solution.py:590
  42.9 0.8 %shard_map.113 = (f32[1,2,8,64,128]{4,3,2,1,0:T(8,128)}, f32[8,2,128]{2,1,0:T(2,128)}, f32[8,2,128]{2,1,0:T(2,128)}) custom-call(f32[1,2,8,64,128]{4,3,2,1,0:T(8,128)S(1)} %get-tuple-element.6.refs_0_, f32[8,2,128]{2,1,0:T(2,128)S(1)} %get-tuple-element.7.refs_1_, f32[8,2,128]{2,1,0:T(2,128)S(1)} %get-tuple-element.8.refs_2_), custom_call_target="tpu_custom_call" | custom-call | tf_op jit(solution)/shard_map/pallas_call | solution.py:651
